TPU v7x, 256 devices: a whole 4x4x8 slice. The times are simulated.
256 devices in a mesh: rows: 16 (over y, x), feat: 16 (over z, core).
Axes of the slice: x: 4, y: 4, z: 8, core: 2. Of those that a mesh axis runs over, the one named last changes fastest.
Arguments:
- feature_bins: int32 [512, 131072], P('feat', 'rows'), may hold values from 0 to 127
- leaf_index: int32 [131072], P('rows'), may hold values from 0 to 63
- doc_scores: float32 [131072], P('rows'), may hold values from -8 to 256
- doc_weights: float32 [131072], P('rows'), may hold values from 0.3 to 3
- destination: int32 [131072], P('rows'), may hold values from 0 to 131071, as said below
- query_ids: int32 [131072], P('rows'), may hold values from 0 to 131071, as said below
- clicks: int32 [131072], P('rows'), may hold values 0 or 1
Outputs:
- histograms: float32 [64, 512, 2, 128], P('rows', 'feat')
Inputs may be any that keep to these rules, and one draw needn't show every extreme that they name: A permutation of the slots; document i goes to owner destination // 8192, slot destination % 8192; each device's 8192 documents hold exactly 512 for every owner. `query_ids`: a query's id is the number of its last slot; each query's slots are consecutive, lie in one aligned block of 256 slots and hold 1 to 256 slots; every owner's slots hold a query of exactly 256.
All inputs are finite; a program needn't handle non-finite values. No bound on the sum of `clicks` on one device may be relied on, other than what follows from the above.
Results may differ from a plain program's by a relative error of at most 0.0023.
Values may be sent and summed in bfloat16 or wider, within the bound.
No kernel may reach another device: no remote copies, remote signals or barrier semaphores. Data moves between devices by JAX's collectives and lax.ppermute only.
A program may use at most 64 MiB of HBM per device.

v0:
```python
import math

import jax
import jax.numpy as jnp
from jax import lax
from jax.sharding import PartitionSpec as P

BINS = 128
LEAVES = 64
QBLOCK = 256


def block_gradients(approx, weight, query_block, target):
    same_query = query_block[:, None] == query_block[None, :]
    query_top = jnp.max(jnp.where(same_query, approx[None, :], -jnp.inf), axis=1)
    scaled = weight * jnp.exp(approx - query_top)
    matrix = same_query.astype(jnp.float32)
    denominator = jnp.dot(matrix, scaled, precision=lax.Precision.HIGHEST)
    clicked = jnp.dot(matrix, weight * target, precision=lax.Precision.HIGHEST)
    chance = scaled / denominator
    gradient = (weight * target - clicked * chance).astype(jnp.bfloat16)
    curvature = (clicked * chance * (1.0 - chance)).astype(jnp.bfloat16)
    return (gradient, curvature)


def query_gradients(approx, weight, query_ids, clicks):
    doc_count = approx.shape[0]
    nblocks = doc_count // QBLOCK
    per_step = 2
    shaped = lambda arr: arr.reshape(nblocks // per_step, per_step, QBLOCK)
    target = clicks.astype(jnp.float32)

    def step_blocks(inputs):
        return jax.vmap(block_gradients)(*inputs)

    gradient, curvature = lax.map(
        step_blocks, (shaped(approx), shaped(weight), shaped(query_ids), shaped(target))
    )
    return jnp.stack([gradient.reshape(doc_count), curvature.reshape(doc_count)])


def shards(feature_bins, leaf_index, doc_scores, doc_weights, destination, query_ids, clicks):
    owners = lax.axis_size("rows")
    doc_count = destination.shape[0]
    capacity = doc_count // owners
    ranking = jnp.argsort(destination)
    sorted_dest = destination[ranking]
    values = jnp.stack([doc_scores[ranking], doc_weights[ranking]]).reshape(2, owners, capacity)
    slot_ids = (sorted_dest % doc_count).reshape(owners, capacity)
    arrived = lax.all_to_all(values, "rows", split_axis=1, concat_axis=1, tiled=True)
    slot_in = lax.all_to_all(slot_ids, "rows", split_axis=0, concat_axis=0, tiled=True)
    owner_values = (
        jnp.zeros((2, doc_count), jnp.float32)
        .at[:, slot_in.reshape(-1)]
        .set(arrived.reshape(2, doc_count))
    )
    owner_stats = query_gradients(owner_values[0], owner_values[1], query_ids, clicks)
    outgoing = owner_stats[:, slot_in]
    returned = lax.all_to_all(outgoing, "rows", split_axis=1, concat_axis=1, tiled=True)
    doc_stats = (
        jnp.zeros((2, doc_count), jnp.bfloat16).at[:, ranking].set(returned.reshape(2, doc_count))
    )
    stats_rows = doc_stats.T
    f_dev = feature_bins.shape[0]
    bunch_size = math.gcd(4, f_dev)
    columns = feature_bins.reshape(f_dev // bunch_size, bunch_size, doc_count)
    bin_range = jnp.arange(BINS, dtype=jnp.int32)
    share = LEAVES // owners
    leaf_hot = (leaf_index[:, None] == jnp.arange(LEAVES, dtype=jnp.int32)[None, :]).astype(
        jnp.bfloat16
    )
    spread = (leaf_hot[:, :, None] * stats_rows[:, None, :]).reshape(doc_count, LEAVES * 2)

    def per_bunch(bunch):
        one_hot = (bunch[:, :, None] == bin_range).astype(jnp.bfloat16)
        return jnp.einsum("gdb,dk->gkb", one_hot, spread, preferred_element_type=jnp.float32)

    pieces = lax.map(per_bunch, columns).reshape(f_dev, LEAVES, 2, BINS)
    summed = lax.psum(jnp.transpose(pieces, (1, 0, 2, 3)), "rows")
    return lax.dynamic_slice_in_dim(summed, lax.axis_index("rows") * share, share, 0)


def solution(mesh):
    placed = (P("feat", "rows"), P("rows"), P("rows"), P("rows"), P("rows"), P("rows"), P("rows"))
    return jax.shard_map(
        shards, mesh=mesh, in_specs=placed, out_specs=P("rows", "feat", None, None), check_vma=False
    )
```

profile of v0, /device:TPU:160, one launch (start us, length us, event | category | flops | bytes accessed | tf_op | source)
XLA Modules:
  0.0 487.3 jit_solution(7182979089565845534)
XLA Ops:
  6.5 7.6 %sort.17 = (s32[8192]{0:T(1024)}, s32[8192]{0:T(1024)S(1)}) sort(s32[8192]{0:T(1024)} %param.15, s32[8192]{0:T(1024)S(1)} %iota.15), dimensions={0}, to_apply=%region_0.0 | sort | flops 106496 | bytes 131072 | tf_op jit(solution)/shard_map/jit(argsort)/sort | solution.py:46
  14.2 45.5 %gather_fusion = s32[8192]{0:T(1024)S(1)} fusion(s32[8192]{0:T(1024)S(1)} %copy-done.1, s32[8192]{0:T(1024)S(1)} %get-tuple-element.140), kind=kCustom, calls=%fused_computation | custom fusion | bytes 98304 | tf_op jit(solution)/shard_map/gather | solution.py:47
  60.4 7.0 %all-to-all-start = ((s32[16,1,512]{2,1,0:T(1,128)}), s32[16,1,512]{2,1,0:T(1,128)S(1)}, u32[]{:S(2)}, u32[]{:S(2)}) async-start(s32[16,1,512]{2,1,0:T(1,128)} %and_select_fusion), calls=%async_computation | async-start | bytes 65536 | tf_op jit(solution)/shard_map/all_to_all | solution.py:51
  67.4 45.5 %gather_fusion.1 = f32[8192]{0:T(1024)S(1)} fusion(f32[8192]{0:T(1024)S(1)} %copy-done, s32[8192]{0:T(1024)S(1)} %get-tuple-element.140), kind=kCustom, calls=%fused_computation.1 | custom fusion | bytes 98304 | tf_op jit(solution)/shard_map/gather | solution.py:48
  113.8 45.5 %gather_fusion.2 = f32[8192]{0:T(1024)S(1)} fusion(f32[8192]{0:T(1024)S(1)} %copy-done.2, s32[8192]{0:T(1024)S(1)} %get-tuple-element.140), kind=kCustom, calls=%fused_computation.2 | custom fusion | bytes 98304 | tf_op jit(solution)/shard_map/gather | solution.py:48
  160.1 7.2 %all-to-all-start.1 = ((f32[2,16,512]{2,0,1:T(2,128)}), f32[2,16,512]{2,0,1:T(2,128)S(1)}, u32[]{:S(2)}, u32[]{:S(2)}) async-start(f32[2,16,512]{2,0,1:T(2,128)} %copy.32), calls=%async_computation.1 | async-start | bytes 131072 | tf_op jit(solution)/shard_map/all_to_all | solution.py:50
  167.4 7.6 %all-to-all-done.1 = f32[2,16,512]{2,0,1:T(2,128)S(1)} async-done(((f32[2,16,512]{2,0,1:T(2,128)}), f32[2,16,512]{2,0,1:T(2,128)S(1)}, u32[]{:S(2)}, u32[]{:S(2)}) %all-to-all-start.1) | async-done | bytes 65568 | tf_op jit(solution)/shard_map/all_to_all | solution.py:50
  177.6 23.0 %scatter_custom_fusion = f32[2,8192]{0,1:T(8,128)} fusion(s32[8192]{0:T(1024)S(1)} %bitcast.107, f32[8192,2]{1,0:T(8,128)} %copy.33, f32[]{:T(128)} %constant.54.clone.1), kind=kCustom, calls=%fused_computation.44 | custom fusion | bytes 66048 | tf_op jit(solution)/shard_map/scatter | solution.py:55
  200.6 6.8 %slice_reduce_fusion = (f32[8192]{0:T(1024)S(1)}, f32[8192]{0:T(1024)S(1)}) fusion(f32[2,8192]{0,1:T(8,128)} %scatter_custom_fusion), kind=kLoop, calls=%fused_computation.42 | loop fusion | bytes 131072 | tf_op jit(solution)/shard_map/slice | solution.py:57
  207.5 18.5 %while.23 = (s32[]{:T(128)}, bf16[16,2,256]{2,1,0:T(2,128)(2,1)S(1)}, bf16[16,2,256]{2,1,0:T(2,128)(2,1)S(1)}, f32[16,2,256]{2,1,0:T(2,128)S(1)}, f32[16,2,256]{...) while((s32[]{:T(128)}, bf16[16,2,256]{2,1,0:T(2,128)(2,1)S(1)}, ...), condition=%wide.region_4.5_spmd, body=%wide.region_2.4_spmd.sunk | while | flops 3806722 | bytes 57449 | solution.py:36
  227.2 29.2 %gather_fusion.3 = bf16[8192,2]{1,0:T(8,128)(2,1)} fusion(bf16[2,8192]{0,1:T(8,128)(2,1)S(1)} %copy.34, s32[8192]{0:T(1024)S(1)} %broadcast_clamp_fusion), kind=kCustom, calls=%fused_computation.3 | custom fusion | bytes 98304 | tf_op jit(solution)/shard_map/gather | solution.py:58
  259.1 3.5 all-to-all-start.2
  264.1 6.0 %all-to-all-done.2 = bf16[2,16,512]{2,0,1:T(2,128)(2,1)S(1)} async-done(((bf16[2,16,512]{2,0,1:T(2,128)(2,1)}), bf16[2,16,512]{2,0,1:T(2,128)(2,1)S(1)}, u32[]{:S(2)}, u32[]{:S(2)}) %all-to-all-start.2) | async-done | bytes 32800 | tf_op jit(solution)/shard_map/all_to_all | solution.py:59
  272.0 22.1 %scatter_custom_fusion.1 = bf16[2,8192]{0,1:T(8,128)(2,1)S(1)} fusion(s32[8192]{0:T(1024)S(1)} %get-tuple-element.141, bf16[8192,2]{1,0:T(8,128)(2,1)} %copy.36, bf16[]{:T(256)} %constant.55.clone.1), kind=kCustom, calls=%fused_computation.48 | custom fusion | bytes 33280 | tf_op jit(solution)/shard_map/scatter | solution.py:61
  295.0 85.1 %while.24 = (s32[]{:T(128)}, f32[8,4,128,128]{3,2,1,0:T(8,128)}, s32[8,4,8192]{2,1,0:T(4,128)}, bf16[8192,2]{0,1:T(2,128)(2,1)S(1)}, bf16[8192,64]{0,1:T(8,128)(2,1)S(1)}, /*index=5*/s32[]{:T(128)}) while((s32[]{:T(128)}, f32[8,4,128,128]{3,2,1,0:T(8,128)}, s32[8,4,8192]{2,1,0:T(4,128)}, bf16[8192,2]{0,1:T(2,128)(2,1)S(1)}, ...), condition=%wide.region_7.8_spmd.clone, body=%wide.region_6.7_spmd.clone.sunk | while | flops 1078984704 | bytes 11174473 | solution.py:78
  300.4 4.4 fusion.47
  311.0 4.4 fusion.47
  321.7 4.4 fusion.47
  332.3 4.4 fusion.47
  342.9 4.4 fusion.47
  353.6 4.4 fusion.47
  364.2 4.4 fusion.47
  374.8 4.4 fusion.47
  380.1 98.7 %all-reduce.2.cloned.1.call-done = f32[64,32,2,128]{3,2,0,1:T(2,128)} async-done(((f32[64,32,2,128]{3,2,0,1:T(2,128)}), f32[64,32,2,128]{3,2,0,1:T(2,128)}) %all-reduce.2.cloned.1.call-update) | async-done | bytes 2097168 | tf_op jit(solution)/shard_map/psum | solution.py:79
  (215 shorter events, 82.3 us)
Async XLA Ops:
  6.5 60.9 %copy-start = (f32[8192]{0:T(1024)S(1)}, f32[8192]{0:T(1024)}, u32[]{:S(2)}) copy-start(f32[8192]{0:T(1024)} %param.13) | copy-start | bytes 98308
  6.5 7.6 %copy-start.1 = (s32[8192]{0:T(1024)S(1)}, s32[8192]{0:T(1024)}, u32[]{:S(2)}) copy-start(s32[8192]{0:T(1024)} %param.15) | copy-start | bytes 98308
  60.4 99.7 %all-to-all-start = ((s32[16,1,512]{2,1,0:T(1,128)}), s32[16,1,512]{2,1,0:T(1,128)S(1)}, u32[]{:S(2)}, u32[]{:S(2)}) async-start(s32[16,1,512]{2,1,0:T(1,128)} %and_select_fusion), calls=%async_computation | async-start | bytes 65536 | tf_op jit(solution)/shard_map/all_to_all | solution.py:51
  113.0 0.8 copy-start.2
  113.8 46.3 %copy-start.5 = (s32[8192]{0:T(1024)S(1)}, s32[8192]{0:T(1024)}, u32[]{:S(2)}) copy-start(s32[8192]{0:T(1024)} %param.17) | copy-start | bytes 98308
  113.8 46.3 %copy-start.6 = (s32[8192]{0:T(1024)S(1)}, s32[8192]{0:T(1024)}, u32[]{:S(2)}) copy-start(s32[8192]{0:T(1024)} %param.16) | copy-start | bytes 98308
  160.1 14.9 %all-to-all-start.1 = ((f32[2,16,512]{2,0,1:T(2,128)}), f32[2,16,512]{2,0,1:T(2,128)S(1)}, u32[]{:S(2)}, u32[]{:S(2)}) async-start(f32[2,16,512]{2,0,1:T(2,128)} %copy.32), calls=%async_computation.1 | async-start | bytes 131072 | tf_op jit(solution)/shard_map/all_to_all | solution.py:50
  226.1 36.5 %copy-start.4 = (s32[8192]{0:T(1024)S(1)}, s32[8192]{0:T(1024)}, u32[]{:S(2)}) copy-start(s32[8192]{0:T(1024)} %param.12) | copy-start | bytes 98308
  227.2 35.6 %copy-start.3 = (s32[32,8192]{1,0:T(8,128)S(1)}, s32[32,8192]{1,0:T(8,128)}, u32[]{:S(2)}) copy-start(s32[32,8192]{1,0:T(8,128)} %param.11) | copy-start | bytes 3145732
  259.1 11.0 %all-to-all-start.2 = ((bf16[2,16,512]{2,0,1:T(2,128)(2,1)}), bf16[2,16,512]{2,0,1:T(2,128)(2,1)S(1)}, u32[]{:S(2)}, u32[]{:S(2)}) async-start(bf16[2,16,512]{2,0,1:T(2,128)(2,1)} %bitcast.18), calls=%async_computation.2 | async-start | bytes 65536 | tf_op jit(solution)/shard_map/all_to_all | solution.py:59
  262.6 216.3 %all-reduce.2.cloned.1.call-start = ((), (), s32[]{:S(2)}) async-start(), calls=%async_computation.3 | async-start | bytes 4194304 | tf_op jit(solution)/shard_map/psum | solution.py:79
Sparse Core Ops, SparseCore 0:
  380.3 98.5 all-reduce.1
where the time goes:
time: 490 us; the launch traced here: 487 us
  local copies, waits for them, and re-layouts  264 us (54%)
  waiting for transfers between devices  112 us (23%)
  matrix products  47.3 us (10%)
  other arithmetic  31.6 us (6%)
  starting transfers between devices  17.8 us (4%)
  between operations  13.7 us (3%)
    psum x1, waiting for transfers between devices, shards(): summed = lax.psum(jnp.transpose(pieces, (1, 0, 2, 3)), 'rows')  98.7 us
    gather x1, local copies, waits for them, and re-layouts, shards(): sorted_dest = destination[ranking]  45.5 us
    gather x1, local copies, waits for them, and re-layouts, shards(): doc_scores[ranking]  45.5 us
    gather x1, local copies, waits for them, and re-layouts, shards(): doc_weights[ranking]  45.5 us
    dot_general x8, matrix products, per_bunch(): jnp.einsum('gdb,dk->gkb', one_hot, spread, preferred_element_type=jnp.flo...  35 us
    gather x2, local copies, waits for them, and re-layouts, shards(): outgoing = owner_stats[:, slot_in]  31.8 us
    scatter x1, local copies, waits for them, and re-layouts, shards(): owner_values = jnp.zeros((2, doc_count), jnp.float32).at[:, slot_in.resha...  23 us
    scatter x1, local copies, waits for them, and re-layouts, shards(): jnp.zeros((2, doc_count), jnp.bfloat16).at[:, ranking]  22.1 us
  transfers between devices with their start and end apart: 4, of which 3 were waited for; matrix products, arithmetic and copies ran while one was open for 19% of the time, Pallas kernels for 0%

commit v1 on v0

v1 whole, which is shorter than its diff:
```python
import jax
import jax.numpy as jnp
from jax import lax
from jax.experimental import pallas as pl
from jax.experimental.pallas import tpu as pltpu
from jax.sharding import PartitionSpec as P

BINS = 128
LEAVES = 64
QBLOCK = 256
OWNERS = 16
DOC = 8192
F_DEV = 32
CH = 1024
F32 = jnp.float32
BF16 = jnp.bfloat16
I32 = jnp.int32


def nt(a, b):
    return lax.dot_general(a, b, (((1,), (1,)), ((), ())), preferred_element_type=F32)


def nn(a, b):
    return lax.dot_general(a, b, (((1,), (0,)), ((), ())), preferred_element_type=F32)


def lanes(tile):
    return jnp.concatenate([tile[r : r + 1, :] for r in range(tile.shape[0])], axis=1)


def rows16(row):
    return jnp.broadcast_to(row.astype(F32), (16, row.shape[1])).astype(BF16)


def iota_bf16(shape, fn):
    parts = [lax.broadcasted_iota(I32, shape, d) for d in range(len(shape))]
    return fn(*parts).astype(F32).astype(BF16)


def split3(x):
    a = x.astype(BF16).astype(F32)
    r = x - a
    b = r.astype(BF16).astype(F32)
    return a, b, r - b


def one_hot(row, width, cols):
    it = iota_bf16((width // 16, 16, cols), lambda g, s, c: g * 16 + s)
    hit = it == rows16(row)[None]
    one = jnp.ones((), BF16)
    zero = jnp.zeros((), BF16)
    return jnp.where(hit, one, zero).reshape(width, cols)


def route_body(dest_ref, score_ref, weight_ref, send_ref, pos_ref, a_ref, b_ref):
    dest = dest_ref[...]
    owner = dest >> 13
    masks = jnp.concatenate(
        [jnp.where(owner == o, 1.0, 0.0).astype(F32) for o in range(OWNERS)], axis=0
    ).astype(BF16)
    r = lax.broadcasted_iota(I32, (128, 256), 0)
    c = lax.broadcasted_iota(I32, (128, 256), 1)
    tri = jnp.where((r < c) | (c >= 128), 1.0, 0.0).astype(F32).astype(BF16)
    counts = nn(masks, tri)
    prefix = counts[:, :128]
    totals = counts[:, 128:].astype(BF16)
    wide = jnp.concatenate([totals[o * 64 : (o + 1) * 64] for o in range(OWNERS)], axis=1)
    r = lax.broadcasted_iota(I32, (64, 64), 0)
    c = lax.broadcasted_iota(I32, (64, 64), 1)
    low = jnp.where(c < r, 1.0, 0.0).astype(F32).astype(BF16)
    before = nn(low, wide)
    rank = jnp.zeros((64, 128), F32)
    for o in range(OWNERS):
        here = prefix[o * 64 : (o + 1) * 64] + before[:, o * 128 : (o + 1) * 128]
        rank = jnp.where(owner == o, here, rank)
    pos_ref[...] = owner * 512 + rank.astype(I32)

    sub = lax.broadcasted_iota(I32, (8, CH), 0)
    target = iota_bf16((8, 16, CH), lambda g, s, c: (g * 2 + s // 8) * 2 + s % 2)

    def chunk(t, carry):
        rows = pl.ds(pl.multiple_of(t * 8, 8), 8)
        cols = pl.ds(pl.multiple_of(t * CH, CH), CH)
        pos = lanes(pos_ref[rows, :])
        slot = lanes(dest_ref[rows, :]) & (DOC - 1)
        s3 = split3(lanes(score_ref[rows, :]))
        w3 = split3(lanes(weight_ref[rows, :]))
        d3 = ((slot & 8128).astype(F32), (slot & 63).astype(F32), jnp.zeros((1, CH), F32))
        b_ref[:, cols] = one_hot(pos & 255, 256, CH)
        hit = target == rows16(pos >> 8)[None]
        for p in range(3):
            full = lambda v: jnp.broadcast_to(v, (8, CH))
            vals = jnp.where(sub < 2, full(s3[p]), jnp.where(sub < 4, full(w3[p]), full(d3[p])))
            both = jnp.concatenate([vals, vals], axis=0).astype(BF16)
            a_ref[p * 128 : (p + 1) * 128, cols] = jnp.where(
                hit, both[None], jnp.zeros((), BF16)
            ).reshape(128, CH)
        return carry

    lax.fori_loop(0, DOC // CH, chunk, 0)
    table = nt(a_ref[...], b_ref[...])
    send_ref[...] = (table[0:128] + table[128:256] + table[256:384]).reshape(OWNERS, 8, 256)


def route(dest, score, weight):
    return pl.pallas_call(
        route_body,
        out_shape=(
            jax.ShapeDtypeStruct((OWNERS, 8, 256), F32),
            jax.ShapeDtypeStruct((64, 128), I32),
        ),
        scratch_shapes=[pltpu.VMEM((384, DOC), BF16), pltpu.VMEM((256, DOC), BF16)],
        name="route",
    )(dest, score, weight)


def owner_body(rec_ref, query_ref, clicks_ref, out_ref, a_ref, b_ref, h_ref):
    def chunk(o, carry):
        tile = rec_ref[o]
        cols = pl.ds(pl.multiple_of(o * 512, 512), 512)
        pick = lambda n: jnp.concatenate([tile[2 * n : 2 * n + 1], tile[2 * n + 1 : 2 * n + 2]], axis=1)
        slot = pick(2).astype(I32)
        b_ref[:, cols] = one_hot(slot & 255, 256, 512)
        block = slot >> 8
        h_ref[pl.ds(o, 1), :] = block
        it = iota_bf16((2, 16, 512), lambda g, s, c: g * 16 + s)
        hit = it == rows16(block)[None]
        for n in range(2):
            for p, v in enumerate(split3(pick(n))):
                at = (p * 2 + n) * 32
                a_ref[at : at + 32, cols] = jnp.where(
                    hit, rows16(v)[None], jnp.zeros((), BF16)
                ).reshape(32, 512)
        return carry

    lax.fori_loop(0, OWNERS, chunk, 0)
    table = nt(a_ref[...], b_ref[...])
    table = table[0:64] + table[64:128] + table[128:192]
    score = table[0:32]
    weight = table[32:64]

    def wide(ref):
        return jnp.concatenate([ref[pl.ds(0, 32, stride=2), :], ref[pl.ds(1, 32, stride=2), :]], axis=1)

    query = wide(query_ref)
    clicks = wide(clicks_ref)
    lane = lax.broadcasted_iota(I32, (32, 256), 1)
    first = lane
    same = []
    for k in range(8):
        d = 1 << k
        same.append((pltpu.roll(query, d, 1) == query) & (lane >= d))

    def scan(x, op):
        for k in range(8):
            d = 1 << k
            x = jnp.where(same[k], op(x, pltpu.roll(x, d, 1)), x)
        return x

    back = []
    for k in range(8):
        d = 1 << k
        back.append((pltpu.roll(query, 256 - d, 1) == query) & (lane < 256 - d))

    def spread(x, op):
        for k in range(8):
            d = 1 << k
            x = jnp.where(back[k], op(x, pltpu.roll(x, 256 - d, 1)), x)
        return x

    last = (query & 255) == lane
    top = spread(scan(score, jnp.maximum), jnp.maximum)
    scaled = weight * jnp.exp(score - top)
    gain = weight * clicks.astype(F32)
    total = lambda x: spread(jnp.where(last, scan(x, jnp.add), 0.0), jnp.add)
    denominator = total(scaled)
    clicked = total(gain)
    chance = scaled / denominator
    gradient = (gain - clicked * chance).astype(BF16)
    curvature = (clicked * chance * (1.0 - chance)).astype(BF16)
    stats = jnp.concatenate([gradient, curvature], axis=0)
    picked = nn(stats, b_ref[...])
    sub = lax.broadcasted_iota(I32, (32, 128), 0)
    for o in range(OWNERS):
        rows = []
        for q in range(4):
            at = o * 512 + q * 128
            hit = sub == h_ref[o : o + 1, q * 128 : (q + 1) * 128]
            for k in range(2):
                part = picked[k * 32 : (k + 1) * 32, at : at + 128]
                rows.append(jnp.sum(jnp.where(hit, part, 0.0), axis=0, keepdims=True))
        out_ref[o] = jnp.concatenate(rows, axis=0)


def owner(rec, query, clicks):
    return pl.pallas_call(
        owner_body,
        out_shape=jax.ShapeDtypeStruct((OWNERS, 8, 128), F32),
        scratch_shapes=[
            pltpu.VMEM((192, DOC), BF16),
            pltpu.VMEM((256, DOC), BF16),
            pltpu.VMEM((OWNERS, 512), I32),
        ],
        name="owner",
    )(rec, query, clicks)


def hist_body(back_ref, pos_ref, leaf_ref, bins_ref, send_ref, spread_ref):
    table = back_ref[...].reshape(128, 128).astype(BF16)

    def expand(t, carry):
        rows = pl.ds(pl.multiple_of(t * 8, 8), 8)
        pos = lanes(pos_ref[rows, :])
        leaf = lanes(leaf_ref[rows, :])
        picked = nn(table, one_hot(pos & 127, 128, CH))
        hi = jnp.broadcast_to(pos >> 7, (8, CH))
        quarter = lax.broadcasted_iota(I32, (8, CH), 0) // 2
        acc = jnp.zeros((8, CH), F32)
        for o in range(OWNERS):
            acc = acc + jnp.where(hi == quarter + 4 * o, picked[o * 8 : (o + 1) * 8], 0.0)
        acc = acc + pltpu.roll(acc, 4, 0)
        acc = acc + pltpu.roll(acc, 2, 0)
        both = jnp.concatenate([acc, acc], axis=0).astype(BF16)
        it = iota_bf16((8, 16, CH), lambda g, s, c: g * 8 + s // 2)
        spread_ref[:, pl.ds(pl.multiple_of(t * CH, CH), CH)] = jnp.where(
            it == rows16(leaf)[None], both[None], jnp.zeros((), BF16)
        ).reshape(128, CH)
        return carry

    lax.fori_loop(0, DOC // CH, expand, 0)

    def pair(p, carry):
        def part(t, acc):
            cols = pl.ds(pl.multiple_of(t * CH, CH), CH)
            hot = jnp.concatenate(
                [one_hot(bins_ref[pl.ds(2 * p + j, 1), cols], 128, CH) for j in range(2)], axis=0
            )
            return acc + nt(spread_ref[:, cols], hot)

        acc = lax.fori_loop(0, DOC // CH, part, jnp.zeros((128, 256), F32))
        left = acc[:, :128].reshape(OWNERS, 1, 8, 128)
        right = acc[:, 128:].reshape(OWNERS, 1, 8, 128)
        send_ref[:, pl.ds(p, 1)] = (
            jnp.concatenate([left, right], axis=1).reshape(OWNERS, 1, 16, 128).astype(BF16)
        )
        return carry

    lax.fori_loop(0, F_DEV // 2, pair, 0)


def hist(back, pos, leaf, bins):
    return pl.pallas_call(
        hist_body,
        out_shape=jax.ShapeDtypeStruct((OWNERS, F_DEV // 2, 16, 128), BF16),
        scratch_shapes=[pltpu.VMEM((128, DOC), BF16)],
        name="hist",
    )(back, pos, leaf, bins)


def total_body(rec_ref, out_ref):
    for p in range(F_DEV // 2):
        acc = rec_ref[0, p].astype(F32)
        for o in range(1, OWNERS):
            acc = acc + rec_ref[o, p].astype(F32)
        for j in range(2):
            for l in range(4):
                out_ref[l, 4 * p + 2 * j : 4 * p + 2 * j + 2, :] = acc[8 * j + 2 * l : 8 * j + 2 * l + 2]


def total(rec):
    return pl.pallas_call(
        total_body, out_shape=jax.ShapeDtypeStruct((4, 2 * F_DEV, 128), F32), name="total"
    )(rec)


def shards(feature_bins, leaf_index, doc_scores, doc_weights, destination, query_ids, clicks):
    tall = lambda a: a.reshape(64, 128)
    swap = lambda a: lax.all_to_all(a, "rows", split_axis=0, concat_axis=0, tiled=True)
    send, pos = route(tall(destination), tall(doc_scores), tall(doc_weights))
    back = owner(swap(send), tall(query_ids), tall(clicks))
    parts = hist(swap(back), pos, tall(leaf_index), feature_bins)
    return total(swap(parts)).reshape(4, F_DEV, 2, BINS)


def solution(mesh):
    placed = (P("feat", "rows"), P("rows"), P("rows"), P("rows"), P("rows"), P("rows"), P("rows"))
    return jax.shard_map(
        shards, mesh=mesh, in_specs=placed, out_specs=P("rows", "feat", None, None), check_vma=False
    )
```

time: 490 us -> 108 us (0.22)
  local copies, waits for them, and re-layouts: 264 us -> 0 us
  waiting for transfers between devices: 112 us -> 0 us
  Pallas kernels: 0 us -> 60.8 us
  matrix products: 47.3 us -> 0 us
  blocking collectives: 0 us -> 46.2 us
  other arithmetic: 31.6 us -> 0 us
  starting transfers between devices: 17.8 us -> 0 us
  between operations: 13.7 us -> 0.01 us
    gather x5 -> x0, local copies, waits for them, and re-layouts: 168 us -> none  [the longest x1 45.5 us: shards(): sorted_dest = destination[ranking]]
    psum x1 -> x0, waiting for transfers between devices: 98.7 us -> none  [shards(): summed = lax.psum(jnp.transpose(pieces, (1, 0, 2, 3)), 'rows')]
    pallas_call x0 -> x4, Pallas kernels: none -> 60.8 us  [the longest x1 45.5 us: hist(): pl.pallas_call(hist_body, out_shape=jax.ShapeDtypeStruct((OWNERS, F_DEV /...]
    dot_general x40 -> x0, matrix products: 47.3 us -> none  [the longest x8 35 us: per_bunch(): jnp.einsum('gdb,dk->gkb', one_hot, spread, preferred_element_type=jnp.flo...]
    all_to_all x0 -> x3, blocking collectives: none -> 46.2 us  [shards(): lax.all_to_all(a, 'rows', split_axis=0, concat_axis=0, tiled=True)]
    scatter x2 -> x0, local copies, waits for them, and re-layouts: 45.1 us -> none  [the longest x1 23 us: shards(): owner_values = jnp.zeros((2, doc_count), jnp.float32).at[:, slot_in.resha...]
    mul x8 -> x0, local copies, waits for them, and re-layouts: 17.9 us -> none  [shards(): leaf_hot[:, :, None] * stats_rows[:, None, :]]
    mul x24 -> x0, other arithmetic: 17.9 us -> none  [the longest x8 17.7 us: shards(): leaf_hot[:, :, None] * stats_rows[:, None, :]]
  transfers between devices with their start and end apart: 4 -> 0, of which waited for: 3 -> 0; matrix products, arithmetic and copies ran while one was open for 19% -> 0% of each run, Pallas kernels for 0% -> 0%
where the time goes in v1:
time: 108 us; the launch traced here: 107 us
  Pallas kernels  60.8 us (56%)
  blocking collectives  46.2 us (43%)
    all_to_all x3, blocking collectives, shards(): lax.all_to_all(a, 'rows', split_axis=0, concat_axis=0, tiled=True)  46.2 us
    pallas_call x1, Pallas kernels, hist(): pl.pallas_call(hist_body, out_shape=jax.ShapeDtypeStruct((OWNERS, F_DEV /...  45.5 us
    pallas_call x1, Pallas kernels, owner(): pl.pallas_call(owner_body, out_shape=jax.ShapeDtypeStruct((OWNERS, 8, 128...  7.84 us
    pallas_call x1, Pallas kernels, route(): pl.pallas_call(route_body, out_shape=(jax.ShapeDtypeStruct((OWNERS, 8, 25...  5.38 us

profile of v1, /device:TPU:160, one launch (start us, length us, event | category | flops | bytes accessed | tf_op | source)
XLA Modules:
  0.0 107.0 jit_solution(16609796170467543641)
XLA Ops:
  0.0 5.4 %route.1 = (f32[16,8,256]{2,1,0:T(8,128)}, s32[64,128]{1,0:T(8,128)}) custom-call(s32[64,128]{1,0:T(8,128)} %bitcast.8, f32[64,128]{1,0:T(8,128)} %bitcast.9, f32[64,128]{1,0:T(8,128)} %bitcast.10), custom_call_target="tpu_custom_call" | custom-call | tf_op jit(solution)/shard_map/route/pallas_call | solution.py:107
  5.4 15.1 %all_to_all.15.rec_ref = f32[16,8,256]{2,1,0:T(8,128)} all-to-all(f32[16,8,256]{2,1,0:T(8,128)} %get-tuple-element.7), channel_id=1, replica_groups=mesh['rows'=16,'feat'=16] {'rows'}, dimensions={0} | all-to-all | bytes 262144 | tf_op jit(solution)/shard_map/all_to_all | solution.py:279
  20.5 7.8 %owner.1 = f32[16,8,128]{2,1,0:T(8,128)} custom-call(f32[16,8,256]{2,1,0:T(8,128)} %all_to_all.15.rec_ref, s32[64,128]{1,0:T(8,128)} %bitcast.11, s32[64,128]{1,0:T(8,128)} %bitcast.12), custom_call_target="tpu_custom_call" | custom-call | tf_op jit(solution)/shard_map/owner/pallas_call | solution.py:197
  28.4 11.8 %all_to_all.16.back_ref = f32[16,8,128]{2,1,0:T(8,128)} all-to-all(f32[16,8,128]{2,1,0:T(8,128)} %owner.1), channel_id=1, replica_groups=mesh['rows'=16,'feat'=16] {'rows'}, dimensions={0} | all-to-all | bytes 131072 | tf_op jit(solution)/shard_map/all_to_all | solution.py:279
  40.1 45.5 %hist.1 = bf16[16,16,16,128]{3,2,1,0:T(8,128)(2,1)} custom-call(f32[16,8,128]{2,1,0:T(8,128)} %all_to_all.16.back_ref, s32[64,128]{1,0:T(8,128)} %get-tuple-element.8.pos_ref, s32[64,128]{1,0:T(8,128)} %bitcast.7, s32[32,8192]{1,0:T(8,128)} %bins_ref.1), custom_call_target="tpu_custom_call" | custom-call | tf_op jit(solution)/shard_map/hist/pallas_call | solution.py:253
  85.7 19.3 %all_to_all.17.rec_ref = bf16[16,16,16,128]{3,2,1,0:T(8,128)(2,1)} all-to-all(bf16[16,16,16,128]{3,2,1,0:T(8,128)(2,1)} %hist.1), channel_id=1, replica_groups=mesh['rows'=16,'feat'=16] {'rows'}, dimensions={0} | all-to-all | bytes 2097152 | tf_op jit(solution)/shard_map/all_to_all | solution.py:279
  105.0 2.0 %total.1 = f32[4,64,128]{2,1,0:T(8,128)} custom-call(bf16[16,16,16,128]{3,2,1,0:T(8,128)(2,1)} %all_to_all.17.rec_ref), custom_call_target="tpu_custom_call" | custom-call | tf_op jit(solution)/shard_map/total/pallas_call | solution.py:272

commit v2 on v1

--- a/solution.py
+++ b/solution.py
@@ -206,8 +206,34 @@
     )(rec, query, clicks)
 
 
+F8 = jnp.float8_e4m3fn
+LOW = 16.0
+GF = 4
+
+
+def one_hot8(row, cols):
+    it = (lax.broadcasted_iota(I32, (4, 32, cols), 0) * 32 + lax.broadcasted_iota(I32, (4, 32, cols), 1)).astype(jnp.int8)
+    r = jnp.broadcast_to(row, (32, cols)).astype(jnp.int8)
+    return jnp.where(it == r[None], jnp.ones((), F8), jnp.zeros((), F8)).reshape(128, cols)
+
+
 def hist_body(back_ref, pos_ref, leaf_ref, bins_ref, send_ref, spread_ref):
-    table = back_ref[...].reshape(128, 128).astype(BF16)
+    back = back_ref[...].reshape(128, 128)
+    table = back.astype(BF16)
+    sub8 = lax.broadcasted_iota(I32, (8, 128), 0)
+    peak = jnp.max(jnp.abs(back_ref[...]), axis=0)
+    peak = jnp.max(peak, axis=1, keepdims=True)
+    odd = lax.broadcasted_iota(I32, (8, 1), 0) % 2
+    top0 = jnp.max(jnp.where(odd == 0, peak, 0.0), axis=0, keepdims=True)
+    top1 = jnp.max(jnp.where(odd == 1, peak, 0.0), axis=0, keepdims=True)
+    top = jnp.where(odd == 0, top0, top1)
+    up = jnp.full((8, 1), 2.0**-20, F32)
+    down = jnp.full((8, 1), 2.0**20, F32)
+    for e in (64, 32, 16, 8, 4, 2, 1):
+        fits = top * (up * 2.0**e) <= 448.0
+        up = jnp.where(fits, up * 2.0**e, up)
+        down = jnp.where(fits, down * 2.0**-e, down)
+    up = jnp.broadcast_to(up, (8, CH))
 
     def expand(t, carry):
         rows = pl.ds(pl.multiple_of(t * 8, 8), 8)
@@ -221,39 +247,39 @@
             acc = acc + jnp.where(hi == quarter + 4 * o, picked[o * 8 : (o + 1) * 8], 0.0)
         acc = acc + pltpu.roll(acc, 4, 0)
         acc = acc + pltpu.roll(acc, 2, 0)
-        both = jnp.concatenate([acc, acc], axis=0).astype(BF16)
+        acc = acc * up
+        high = acc.astype(F8).astype(F32)
+        low = (acc - high) * LOW
         it = iota_bf16((8, 16, CH), lambda g, s, c: g * 8 + s // 2)
-        spread_ref[:, pl.ds(pl.multiple_of(t * CH, CH), CH)] = jnp.where(
-            it == rows16(leaf)[None], both[None], jnp.zeros((), BF16)
-        ).reshape(128, CH)
+        hit = it == rows16(leaf)[None]
+        for n, v in enumerate((high, low)):
+            both = jnp.concatenate([v, v], axis=0).astype(BF16)
+            spread_ref[n * 128 : (n + 1) * 128, pl.ds(pl.multiple_of(t * CH, CH), CH)] = (
+                jnp.where(hit, both[None], jnp.zeros((), BF16)).reshape(128, CH).astype(F8)
+            )
         return carry
 
     lax.fori_loop(0, DOC // CH, expand, 0)
-
-    def pair(p, carry):
-        def part(t, acc):
-            cols = pl.ds(pl.multiple_of(t * CH, CH), CH)
-            hot = jnp.concatenate(
-                [one_hot(bins_ref[pl.ds(2 * p + j, 1), cols], 128, CH) for j in range(2)], axis=0
-            )
-            return acc + nt(spread_ref[:, cols], hot)
-
-        acc = lax.fori_loop(0, DOC // CH, part, jnp.zeros((128, 256), F32))
-        left = acc[:, :128].reshape(OWNERS, 1, 8, 128)
-        right = acc[:, 128:].reshape(OWNERS, 1, 8, 128)
-        send_ref[:, pl.ds(p, 1)] = (
-            jnp.concatenate([left, right], axis=1).reshape(OWNERS, 1, 16, 128).astype(BF16)
+    scale = jnp.broadcast_to(down, (8, 128))[None]
+
+    def group(p, carry):
+        hot = jnp.concatenate([one_hot8(bins_ref[pl.ds(GF * p + j, 1), :], DOC) for j in range(GF)], axis=0)
+        acc = nt(spread_ref[...], hot)
+        acc = acc[:128] + acc[128:] * (1.0 / LOW)
+        cut = [(acc[:, 128 * j : 128 * j + 128].reshape(OWNERS, 8, 128) * scale).reshape(OWNERS, 1, 8, 128) for j in range(GF)]
+        send_ref[:, pl.ds(p * (GF // 2), GF // 2)] = (
+            jnp.concatenate(cut, axis=1).reshape(OWNERS, GF // 2, 16, 128).astype(BF16)
         )
         return carry
 
-    lax.fori_loop(0, F_DEV // 2, pair, 0)
+    lax.fori_loop(0, F_DEV // GF, group, 0)
 
 
 def hist(back, pos, leaf, bins):
     return pl.pallas_call(
         hist_body,
         out_shape=jax.ShapeDtypeStruct((OWNERS, F_DEV // 2, 16, 128), BF16),
-        scratch_shapes=[pltpu.VMEM((128, DOC), BF16)],
+        scratch_shapes=[pltpu.VMEM((256, DOC), F8)],
         name="hist",
     )(back, pos, leaf, bins)
 

time: 108 us -> 76.6 us (0.71)
  Pallas kernels: 60.8 us -> 29.9 us
    pallas_call x1, Pallas kernels: 45.5 us -> 14.7 us  [hist(): pl.pallas_call(hist_body, out_shape=jax.ShapeDtypeStruct((OWNERS, F_DEV /...]
where the time goes in v2:
time: 76.6 us; the launch traced here: 76.1 us
  blocking collectives  46.2 us (60%)
  Pallas kernels  29.9 us (39%)
    all_to_all x3, blocking collectives, shards(): lax.all_to_all(a, 'rows', split_axis=0, concat_axis=0, tiled=True)  46.2 us
    pallas_call x1, Pallas kernels, hist(): pl.pallas_call(hist_body, out_shape=jax.ShapeDtypeStruct((OWNERS, F_DEV /...  14.7 us
    pallas_call x1, Pallas kernels, owner(): pl.pallas_call(owner_body, out_shape=jax.ShapeDtypeStruct((OWNERS, 8, 128...  7.84 us
    pallas_call x1, Pallas kernels, route(): pl.pallas_call(route_body, out_shape=(jax.ShapeDtypeStruct((OWNERS, 8, 25...  5.38 us
    pallas_call x1, Pallas kernels, total(): pl.pallas_call(total_body, out_shape=jax.ShapeDtypeStruct((4, 2 * F_DEV,...  2.02 us

profile of v2, /device:TPU:160, one launch (start us, length us, event | category | flops | bytes accessed | tf_op | source)
XLA Modules:
  0.0 76.1 jit_solution(6287977643526236752)
XLA Ops:
  0.0 5.4 %route.1 = (f32[16,8,256]{2,1,0:T(8,128)}, s32[64,128]{1,0:T(8,128)}) custom-call(s32[64,128]{1,0:T(8,128)} %bitcast.8, f32[64,128]{1,0:T(8,128)} %bitcast.9, f32[64,128]{1,0:T(8,128)} %bitcast.10), custom_call_target="tpu_custom_call" | custom-call | tf_op jit(solution)/shard_map/route/pallas_call | solution.py:107
  5.4 15.1 %all_to_all.15.rec_ref = f32[16,8,256]{2,1,0:T(8,128)} all-to-all(f32[16,8,256]{2,1,0:T(8,128)} %get-tuple-element.7), channel_id=1, replica_groups=mesh['rows'=16,'feat'=16] {'rows'}, dimensions={0} | all-to-all | bytes 262144 | tf_op jit(solution)/shard_map/all_to_all | solution.py:305
  20.5 7.8 %owner.1 = f32[16,8,128]{2,1,0:T(8,128)} custom-call(f32[16,8,256]{2,1,0:T(8,128)} %all_to_all.15.rec_ref, s32[64,128]{1,0:T(8,128)} %bitcast.11, s32[64,128]{1,0:T(8,128)} %bitcast.12), custom_call_target="tpu_custom_call" | custom-call | tf_op jit(solution)/shard_map/owner/pallas_call | solution.py:197
  28.4 11.8 %all_to_all.16.back_ref = f32[16,8,128]{2,1,0:T(8,128)} all-to-all(f32[16,8,128]{2,1,0:T(8,128)} %owner.1), channel_id=1, replica_groups=mesh['rows'=16,'feat'=16] {'rows'}, dimensions={0} | all-to-all | bytes 131072 | tf_op jit(solution)/shard_map/all_to_all | solution.py:305
  40.1 14.7 %hist.1 = bf16[16,16,16,128]{3,2,1,0:T(8,128)(2,1)} custom-call(f32[16,8,128]{2,1,0:T(8,128)} %all_to_all.16.back_ref, s32[64,128]{1,0:T(8,128)} %get-tuple-element.8.pos_ref, s32[64,128]{1,0:T(8,128)} %bitcast.7, s32[32,8192]{1,0:T(8,128)} %bins_ref.1), custom_call_target="tpu_custom_call" | custom-call | tf_op jit(solution)/shard_map/hist/pallas_call | solution.py:279
  54.8 19.3 %all_to_all.17.rec_ref = bf16[16,16,16,128]{3,2,1,0:T(8,128)(2,1)} all-to-all(bf16[16,16,16,128]{3,2,1,0:T(8,128)(2,1)} %hist.1), channel_id=1, replica_groups=mesh['rows'=16,'feat'=16] {'rows'}, dimensions={0} | all-to-all | bytes 2097152 | tf_op jit(solution)/shard_map/all_to_all | solution.py:305
  74.1 2.0 %total.1 = f32[4,64,128]{2,1,0:T(8,128)} custom-call(bf16[16,16,16,128]{3,2,1,0:T(8,128)(2,1)} %all_to_all.17.rec_ref), custom_call_target="tpu_custom_call" | custom-call | tf_op jit(solution)/shard_map/total/pallas_call | solution.py:298

commit v3 on v1

v3 whole, which is shorter than its diff:
```python
import jax
import jax.numpy as jnp
from jax import lax
from jax.experimental import pallas as pl
from jax.experimental.pallas import tpu as pltpu
from jax.sharding import PartitionSpec as P

BINS = 128
LEAVES = 64
QBLOCK = 256
OWNERS = 16
DOC = 8192
F_DEV = 32
CH = 1024
F32 = jnp.float32
BF16 = jnp.bfloat16
I32 = jnp.int32


def nt(a, b):
    return lax.dot_general(a, b, (((1,), (1,)), ((), ())), preferred_element_type=F32)


def nn(a, b):
    return lax.dot_general(a, b, (((1,), (0,)), ((), ())), preferred_element_type=F32)


def lanes(tile):
    return jnp.concatenate([tile[r : r + 1, :] for r in range(tile.shape[0])], axis=1)


def rows16(row):
    return jnp.broadcast_to(row.astype(F32), (16, row.shape[1])).astype(BF16)


def iota_bf16(shape, fn):
    parts = [lax.broadcasted_iota(I32, shape, d) for d in range(len(shape))]
    return fn(*parts).astype(F32).astype(BF16)


def split3(x):
    a = x.astype(BF16).astype(F32)
    r = x - a
    b = r.astype(BF16).astype(F32)
    return a, b, r - b


def one_hot(row, width, cols):
    it = iota_bf16((width // 16, 16, cols), lambda g, s, c: g * 16 + s)
    hit = it == rows16(row)[None]
    one = jnp.ones((), BF16)
    zero = jnp.zeros((), BF16)
    return jnp.where(hit, one, zero).reshape(width, cols)


def route_body(dest_ref, score_ref, weight_ref, send_ref, pos_ref, a_ref, b_ref):
    dest = dest_ref[...]
    owner = dest >> 13
    masks = jnp.concatenate(
        [jnp.where(owner == o, 1.0, 0.0).astype(F32) for o in range(OWNERS)], axis=0
    ).astype(BF16)
    r = lax.broadcasted_iota(I32, (128, 256), 0)
    c = lax.broadcasted_iota(I32, (128, 256), 1)
    tri = jnp.where((r < c) | (c >= 128), 1.0, 0.0).astype(F32).astype(BF16)
    counts = nn(masks, tri)
    prefix = counts[:, :128]
    totals = counts[:, 128:].astype(BF16)
    wide = jnp.concatenate([totals[o * 64 : (o + 1) * 64] for o in range(OWNERS)], axis=1)
    r = lax.broadcasted_iota(I32, (64, 64), 0)
    c = lax.broadcasted_iota(I32, (64, 64), 1)
    low = jnp.where(c < r, 1.0, 0.0).astype(F32).astype(BF16)
    before = nn(low, wide)
    rank = jnp.zeros((64, 128), F32)
    for o in range(OWNERS):
        here = prefix[o * 64 : (o + 1) * 64] + before[:, o * 128 : (o + 1) * 128]
        rank = jnp.where(owner == o, here, rank)

    sub = lax.broadcasted_iota(I32, (8, CH), 0)
    target = iota_bf16((8, 16, CH), lambda g, s, c: (g * 2 + s // 8) * 2 + s % 2)

    score = split3(score_ref[...])
    weight = split3(weight_ref[...])
    slot = dest & (DOC - 1)
    zero = jnp.zeros((64, 128), F32)
    fields = (
        (score[0], weight[0], (slot & 8128).astype(F32), score[2]),
        (score[1], weight[1], (slot & 63).astype(F32), zero),
    )
    place = owner * 512 + rank.astype(I32)
    pos_ref[...] = place
    for t in range(DOC // CH):
        rows = slice(t * 8, t * 8 + 8)
        cols = slice(t * CH, t * CH + CH)
        pos = lanes(place[rows])
        b_ref[:, cols] = one_hot(pos & 255, 256, CH)
        hit = target == rows16(pos >> 8)[None]
        for p in range(2):
            part = [jnp.broadcast_to(lanes(v[rows]), (8, CH)) for v in fields[p]]
            vals = jnp.where(
                sub < 4,
                jnp.where(sub < 2, part[0], part[1]),
                jnp.where(sub < 6, part[2], part[3]),
            )
            both = jnp.concatenate([vals, vals], axis=0).astype(BF16)
            a_ref[p * 128 : (p + 1) * 128, cols] = jnp.where(
                hit, both[None], jnp.zeros((), BF16)
            ).reshape(128, CH)
    table = nt(a_ref[...], b_ref[...])
    send_ref[...] = (table[0:128] + table[128:256]).reshape(OWNERS, 8, 256)


def route(dest, score, weight):
    return pl.pallas_call(
        route_body,
        out_shape=(
            jax.ShapeDtypeStruct((OWNERS, 8, 256), F32),
            jax.ShapeDtypeStruct((64, 128), I32),
        ),
        scratch_shapes=[pltpu.VMEM((256, DOC), BF16), pltpu.VMEM((256, DOC), BF16)],
        in_specs=[pl.BlockSpec(memory_space=pltpu.VMEM)] * 3,
        out_specs=(pl.BlockSpec(memory_space=pltpu.VMEM), pl.BlockSpec(memory_space=pltpu.VMEM)),
        compiler_params=pltpu.CompilerParams(vmem_limit_bytes=24 << 20),
        name="route",
    )(dest, score, weight)


def owner_body(rec_ref, query_ref, clicks_ref, out_ref, a_ref, b_ref, h_ref):
    it = iota_bf16((2, 16, 512), lambda g, s, c: g * 16 + s)
    for o in range(OWNERS):
        tile = rec_ref[o]
        cols = slice(o * 512, o * 512 + 512)
        pick = lambda n: jnp.concatenate([tile[2 * n : 2 * n + 1], tile[2 * n + 1 : 2 * n + 2]], axis=1)
        slot = pick(2).astype(I32)
        b_ref[:, cols] = one_hot(slot & 255, 256, 512)
        block = slot >> 8
        h_ref[o : o + 1, :] = block
        hit = it == rows16(block)[None]
        s3 = split3(pick(0) + pick(3))
        w3 = split3(pick(1))
        for n, v in enumerate((s3[0], w3[0], s3[1], w3[1], s3[2])):
            a_ref[n * 32 : n * 32 + 32, cols] = jnp.where(
                hit, rows16(v)[None], jnp.zeros((), BF16)
            ).reshape(32, 512)
    table = nt(a_ref[...], b_ref[...])
    score = table[0:32] + table[64:96] + table[128:160]
    weight = table[32:64] + table[96:128]

    def wide(ref):
        return jnp.concatenate([ref[pl.ds(0, 32, stride=2), :], ref[pl.ds(1, 32, stride=2), :]], axis=1)

    query = wide(query_ref)
    clicks = wide(clicks_ref)
    lane = lax.broadcasted_iota(I32, (32, 256), 1)
    steps = [1 << k for k in range(8)]
    fore = [(pltpu.roll(query, d, 1) == query) & (lane >= d) for d in steps]
    back = [(pltpu.roll(query, 256 - d, 1) == query) & (lane < 256 - d) for d in steps]

    def scans(x, op):
        y = x
        for d, f, b in zip(steps, fore, back):
            x = jnp.where(f, op(x, pltpu.roll(x, d, 1)), x)
            y = jnp.where(b, op(y, pltpu.roll(y, 256 - d, 1)), y)
        return x, y

    top = jnp.maximum(*scans(score, jnp.maximum))
    scaled = weight * jnp.exp(score - top)
    gain = weight * clicks.astype(F32)

    def total(x):
        left, right = scans(x, jnp.add)
        return left + (right - x)

    denominator = total(scaled)
    clicked = total(gain)
    chance = scaled / denominator
    gradient = (gain - clicked * chance).astype(BF16)
    curvature = (clicked * chance * (1.0 - chance)).astype(BF16)
    stats = jnp.concatenate([gradient, curvature], axis=0)
    picked = nn(stats, b_ref[...])
    sub = lax.broadcasted_iota(I32, (32, 128), 0)
    for o in range(OWNERS):
        rows = []
        for q in range(4):
            at = o * 512 + q * 128
            hit = sub == h_ref[o : o + 1, q * 128 : (q + 1) * 128]
            for k in range(2):
                part = picked[k * 32 : (k + 1) * 32, at : at + 128]
                rows.append(jnp.sum(jnp.where(hit, part, 0.0), axis=0, keepdims=True))
        out_ref[o] = jnp.concatenate(rows, axis=0)


def owner(rec, query, clicks):
    return pl.pallas_call(
        owner_body,
        out_shape=jax.ShapeDtypeStruct((OWNERS, 8, 128), F32),
        scratch_shapes=[
            pltpu.VMEM((160, DOC), BF16),
            pltpu.VMEM((256, DOC), BF16),
            pltpu.VMEM((OWNERS, 512), I32),
        ],
        in_specs=[pl.BlockSpec(memory_space=pltpu.VMEM)] * 3,
        out_specs=pl.BlockSpec(memory_space=pltpu.VMEM),
        compiler_params=pltpu.CompilerParams(vmem_limit_bytes=24 << 20),
        name="owner",
    )(rec, query, clicks)


F8 = jnp.float8_e4m3fn
LOW = 16.0
GF = 8
PB = 8


def one_hot8(row, cols):
    it = (lax.broadcasted_iota(I32, (4, 32, cols), 0) * 32 + lax.broadcasted_iota(I32, (4, 32, cols), 1)).astype(jnp.int8)
    r = jnp.broadcast_to(row, (32, cols)).astype(jnp.int8)
    return jnp.where(it == r[None], jnp.ones((), F8), jnp.zeros((), F8)).reshape(128, cols)


def hist_body(back_ref, pos_ref, leaf_ref, bins_ref, send_ref, spread_ref, down_ref):
    @pl.when(pl.program_id(0) == 0)
    def _():
        back = back_ref[...].reshape(128, 128)
        table = back.astype(BF16)
        sub8 = lax.broadcasted_iota(I32, (8, 128), 0)
        peak = jnp.max(jnp.abs(back_ref[...]), axis=0)
        peak = jnp.max(peak, axis=1, keepdims=True)
        odd = lax.broadcasted_iota(I32, (8, 1), 0) % 2
        top0 = jnp.max(jnp.where(odd == 0, peak, 0.0), axis=0, keepdims=True)
        top1 = jnp.max(jnp.where(odd == 1, peak, 0.0), axis=0, keepdims=True)
        top = jnp.where(odd == 0, top0, top1)
        up = jnp.full((8, 1), 2.0**-20, F32)
        down = jnp.full((8, 1), 2.0**20, F32)
        for e in (64, 32, 16, 8, 4, 2, 1):
            fits = top * (up * 2.0**e) <= 448.0
            up = jnp.where(fits, up * 2.0**e, up)
            down = jnp.where(fits, down * 2.0**-e, down)
        up = jnp.broadcast_to(up, (8, CH))

        for t in range(DOC // CH):
            rows = slice(t * 8, t * 8 + 8)
            pos = lanes(pos_ref[rows, :])
            leaf = lanes(leaf_ref[rows, :])
            picked = nn(table, one_hot(pos & 127, 128, CH))
            hi = jnp.broadcast_to(pos >> 7, (8, CH))
            quarter = lax.broadcasted_iota(I32, (8, CH), 0) // 2
            acc = jnp.zeros((8, CH), F32)
            for o in range(OWNERS):
                acc = acc + jnp.where(hi == quarter + 4 * o, picked[o * 8 : (o + 1) * 8], 0.0)
            acc = acc + pltpu.roll(acc, 4, 0)
            acc = acc + pltpu.roll(acc, 2, 0)
            acc = acc * up
            high = acc.astype(F8).astype(F32)
            low = (acc - high) * LOW
            it = iota_bf16((8, 16, CH), lambda g, s, c: g * 8 + s // 2)
            hit = it == rows16(leaf)[None]
            for n, v in enumerate((high, low)):
                both = jnp.concatenate([v, v], axis=0).astype(BF16)
                spread_ref[n * 128 : (n + 1) * 128, t * CH : t * CH + CH] = (
                    jnp.where(hit, both[None], jnp.zeros((), BF16)).reshape(128, CH).astype(F8)
                )
        down_ref[...] = jnp.broadcast_to(down, (8, 128))

    scale = down_ref[...][None]
    hot = jnp.concatenate([one_hot8(bins_ref[j : j + 1, :], DOC) for j in range(GF)], axis=0)
    acc = nt(spread_ref[...], hot)
    acc = acc[:128] + acc[128:] * (1.0 / LOW)
    cut = [
        (acc[:, 128 * j : 128 * j + 128].reshape(OWNERS, 8, 128) * scale).reshape(OWNERS, 1, 8, 128)
        for j in range(GF)
    ]
    send_ref[...] = (
        jnp.concatenate(cut, axis=1).reshape(OWNERS, GF // 2, 16, 128).astype(BF16)
    )


def hist(back, pos, leaf, bins):
    whole = lambda a: pl.BlockSpec(a.shape, lambda p: (0,) * a.ndim)
    return pl.pallas_call(
        hist_body,
        grid=(F_DEV // GF,),
        in_specs=[whole(back), whole(pos), whole(leaf), pl.BlockSpec((GF, DOC), lambda p: (p, 0))],
        out_specs=pl.BlockSpec((OWNERS, GF // 2, 16, 128), lambda p: (0, p, 0, 0)),
        out_shape=jax.ShapeDtypeStruct((OWNERS, F_DEV // 2, 16, 128), BF16),
        scratch_shapes=[pltpu.VMEM((256, DOC), F8), pltpu.VMEM((8, 128), F32)],
        compiler_params=pltpu.CompilerParams(vmem_limit_bytes=40 << 20),
        name="hist",
    )(back, pos, leaf, bins)


def total_body(rec_ref, out_ref):
    for p in range(PB):
        acc = rec_ref[0, p].astype(F32)
        for o in range(1, OWNERS):
            acc = acc + rec_ref[o, p].astype(F32)
        for j in range(2):
            for l in range(4):
                out_ref[l, 4 * p + 2 * j : 4 * p + 2 * j + 2, :] = acc[8 * j + 2 * l : 8 * j + 2 * l + 2]


def total(rec):
    return pl.pallas_call(
        total_body,
        grid=(F_DEV // 2 // PB,),
        in_specs=[pl.BlockSpec((OWNERS, PB, 16, 128), lambda p: (0, p, 0, 0))],
        out_specs=pl.BlockSpec((4, 4 * PB, 128), lambda p: (0, p, 0)),
        out_shape=jax.ShapeDtypeStruct((4, 2 * F_DEV, 128), F32),
        compiler_params=pltpu.CompilerParams(vmem_limit_bytes=16 << 20),
        name="total",
    )(rec)


def shards(feature_bins, leaf_index, doc_scores, doc_weights, destination, query_ids, clicks):
    tall = lambda a: a.reshape(64, 128)
    swap = lambda a: lax.all_to_all(a, "rows", split_axis=0, concat_axis=0, tiled=True)
    send, pos = route(tall(destination), tall(doc_scores), tall(doc_weights))
    back = owner(swap(send), tall(query_ids), tall(clicks))
    parts = hist(swap(back), pos, tall(leaf_index), feature_bins)
    return total(swap(parts)).reshape(4, F_DEV, 2, BINS)


def solution(mesh):
    placed = (P("feat", "rows"), P("rows"), P("rows"), P("rows"), P("rows"), P("rows"), P("rows"))
    return jax.shard_map(
        shards, mesh=mesh, in_specs=placed, out_specs=P("rows", "feat", None, None), check_vma=False
    )
```

time: 108 us -> 65.9 us (0.61)
  Pallas kernels: 60.8 us -> 18.1 us
  local copies, waits for them, and re-layouts: 0 us -> 3.52 us
  blocking collectives: 46.2 us -> 43.7 us
    pallas_call x2, Pallas kernels: 47.6 us -> 11.9 us  [the longest x1 11 us: hist(): pl.pallas_call(hist_body, grid=(F_DEV // GF,), in_specs=[whole(back), who...]
    unnamed x0 -> x14, local copies, waits for them, and re-layouts: none -> 3.52 us
    pallas_call x1, Pallas kernels: 7.84 us -> 4.33 us  [owner(): pl.pallas_call(owner_body, out_shape=jax.ShapeDtypeStruct((OWNERS, 8, 128...]
    pallas_call x1, Pallas kernels: 5.38 us -> 1.91 us  [route(): pl.pallas_call(route_body, out_shape=(jax.ShapeDtypeStruct((OWNERS, 8, 25...]
    all_to_all x3, blocking collectives: 46.2 us -> 43.7 us  [shards(): lax.all_to_all(a, 'rows', split_axis=0, concat_axis=0, tiled=True)]
where the time goes in v3:
time: 65.9 us; the launch traced here: 65.3 us
  blocking collectives  43.7 us (66%)
  Pallas kernels  18.1 us (27%)
  local copies, waits for them, and re-layouts  3.52 us (5%)
    all_to_all x3, blocking collectives, shards(): lax.all_to_all(a, 'rows', split_axis=0, concat_axis=0, tiled=True)  43.7 us
    pallas_call x1, Pallas kernels, hist(): pl.pallas_call(hist_body, grid=(F_DEV // GF,), in_specs=[whole(back), who...  11 us
    pallas_call x1, Pallas kernels, owner(): pl.pallas_call(owner_body, out_shape=jax.ShapeDtypeStruct((OWNERS, 8, 128...  4.33 us
    unnamed x14, local copies, waits for them, and re-layouts  3.52 us
    pallas_call x1, Pallas kernels, route(): pl.pallas_call(route_body, out_shape=(jax.ShapeDtypeStruct((OWNERS, 8, 25...  1.91 us

profile of v3, /device:TPU:160, one launch (start us, length us, event | category | flops | bytes accessed | tf_op | source)
XLA Modules:
  0.0 65.3 jit_solution(14314228462236523538)
XLA Ops:
  0.0 0.0 copy-start.2
  0.0 0.8 %copy-done.2 = s32[8192]{0:T(1024)S(1)} copy-done((s32[8192]{0:T(1024)S(1)}, s32[8192]{0:T(1024)}, u32[]{:S(2)}) %copy-start.2) | copy-done | bytes 32792
  0.8 0.0 copy-start.3
  0.8 0.8 %copy-done.3 = f32[8192]{0:T(1024)S(1)} copy-done((f32[8192]{0:T(1024)S(1)}, f32[8192]{0:T(1024)}, u32[]{:S(2)}) %copy-start.3) | copy-done | bytes 32792
  1.5 0.0 copy-start.4
  1.5 0.8 %copy-done.4 = f32[8192]{0:T(1024)S(1)} copy-done((f32[8192]{0:T(1024)S(1)}, f32[8192]{0:T(1024)}, u32[]{:S(2)}) %copy-start.4) | copy-done | bytes 32792
  2.3 1.9 %route.1 = (f32[16,8,256]{2,1,0:T(8,128)S(1)}, s32[64,128]{1,0:T(8,128)S(1)}) custom-call(s32[64,128]{1,0:T(8,128)S(1)} %bitcast.8, f32[64,128]{1,0:T(8,128)S(1)} %bitcast.9, f32[64,128]{1,0:T(8,128)S(1)} %bitcast.10), custom_call_target="tpu_custom_call" | custom-call | tf_op jit(solution)/shard_map/route/pallas_call | solution.py:113
  4.2 0.0 copy-start.5
  4.2 0.0 copy-start.6
  4.2 14.8 %all_to_all.15.rec_ref = f32[16,8,256]{2,1,0:T(8,128)S(1)} all-to-all(f32[16,8,256]{2,1,0:T(8,128)S(1)} %get-tuple-element.7), channel_id=1, replica_groups=mesh['rows'=16,'feat'=16] {'rows'}, dimensions={0} | all-to-all | bytes 262144 | tf_op jit(solution)/shard_map/all_to_all | solution.py:315
  19.0 0.0 copy-done.5
  19.0 0.0 copy-done.6
  19.0 4.3 %owner.1 = f32[16,8,128]{2,1,0:T(8,128)S(1)} custom-call(f32[16,8,256]{2,1,0:T(8,128)S(1)} %all_to_all.15.rec_ref, s32[64,128]{1,0:T(8,128)S(1)} %bitcast.11, s32[64,128]{1,0:T(8,128)S(1)} %bitcast.12), custom_call_target="tpu_custom_call" | custom-call | tf_op jit(solution)/shard_map/owner/pallas_call | solution.py:193
  23.4 0.0 copy-start.1
  23.4 10.7 %all_to_all.16.back_ref = f32[16,8,128]{2,1,0:T(8,128)S(1)} all-to-all(f32[16,8,128]{2,1,0:T(8,128)S(1)} %owner.1), channel_id=1, replica_groups=mesh['rows'=16,'feat'=16] {'rows'}, dimensions={0} | all-to-all | bytes 131072 | tf_op jit(solution)/shard_map/all_to_all | solution.py:315
  34.1 0.0 copy-done.1
  34.1 0.0 copy-start
  34.1 1.2 %copy-done = s32[32,8192]{1,0:T(8,128)S(1)} copy-done((s32[32,8192]{1,0:T(8,128)S(1)}, s32[32,8192]{1,0:T(8,128)}, u32[]{:S(2)}) %copy-start) | copy-done | bytes 1048600
  35.4 11.0 %hist.1 = bf16[16,16,16,128]{3,2,1,0:T(8,128)(2,1)S(1)} custom-call(f32[16,8,128]{2,1,0:T(8,128)S(1)} %all_to_all.16.back_ref, s32[64,128]{1,0:T(8,128)S(1)} %get-tuple-element.8.pos_ref, s32[64,128]{1,0:T(8,128)S(1)} %bitcast.7, s32[32,8192]{1,0:T(8,128)S(1)} %copy-done), custom_call_target="tpu_custom_call" | custom-call | tf_op jit(solution)/shard_map/hist/pallas_call | solution.py:279
  46.3 18.1 %all_to_all.17.rec_ref = bf16[16,16,16,128]{3,2,1,0:T(8,128)(2,1)S(1)} all-to-all(bf16[16,16,16,128]{3,2,1,0:T(8,128)(2,1)S(1)} %hist.1), channel_id=1, replica_groups=mesh['rows'=16,'feat'=16] {'rows'}, dimensions={0} | all-to-all | bytes 2097152 | tf_op jit(solution)/shard_map/all_to_all | solution.py:315
  64.4 0.9 %total.1 = f32[4,64,128]{2,1,0:T(8,128)} custom-call(bf16[16,16,16,128]{3,2,1,0:T(8,128)(2,1)S(1)} %all_to_all.17.rec_ref), custom_call_target="tpu_custom_call" | custom-call | tf_op jit(solution)/shard_map/total/pallas_call | solution.py:302
Async XLA Ops:
  0.0 0.8 %copy-start.2 = (s32[8192]{0:T(1024)S(1)}, s32[8192]{0:T(1024)}, u32[]{:S(2)}) copy-start(s32[8192]{0:T(1024)} %param.11) | copy-start | bytes 98308
  0.8 0.8 %copy-start.3 = (f32[8192]{0:T(1024)S(1)}, f32[8192]{0:T(1024)}, u32[]{:S(2)}) copy-start(f32[8192]{0:T(1024)} %param.9) | copy-start | bytes 98308
  1.5 0.8 %copy-start.4 = (f32[8192]{0:T(1024)S(1)}, f32[8192]{0:T(1024)}, u32[]{:S(2)}) copy-start(f32[8192]{0:T(1024)} %param.10) | copy-start | bytes 98308
  4.2 14.9 %copy-start.5 = (s32[8192]{0:T(1024)S(1)}, s32[8192]{0:T(1024)}, u32[]{:S(2)}) copy-start(s32[8192]{0:T(1024)} %param.12) | copy-start | bytes 98308
  4.2 14.8 %copy-start.6 = (s32[8192]{0:T(1024)S(1)}, s32[8192]{0:T(1024)}, u32[]{:S(2)}) copy-start(s32[8192]{0:T(1024)} %param.13) | copy-start | bytes 98308
  23.4 10.8 %copy-start.1 = (s32[8192]{0:T(1024)S(1)}, s32[8192]{0:T(1024)}, u32[]{:S(2)}) copy-start(s32[8192]{0:T(1024)} %param.8) | copy-start | bytes 98308
  34.1 1.2 %copy-start = (s32[32,8192]{1,0:T(8,128)S(1)}, s32[32,8192]{1,0:T(8,128)}, u32[]{:S(2)}) copy-start(s32[32,8192]{1,0:T(8,128)} %bins_ref.1) | copy-start | bytes 3145732

commit v4 on v3

--- a/solution.py
+++ b/solution.py
@@ -53,8 +53,8 @@
     return jnp.where(hit, one, zero).reshape(width, cols)
 
 
-def route_body(dest_ref, score_ref, weight_ref, send_ref, pos_ref, a_ref, b_ref):
-    dest = dest_ref[...]
+def route_body(docs_ref, send_ref, pos_ref, a_ref, b_ref):
+    dest = docs_ref[0].astype(I32)
     owner = dest >> 13
     masks = jnp.concatenate(
         [jnp.where(owner == o, 1.0, 0.0).astype(F32) for o in range(OWNERS)], axis=0
@@ -78,8 +78,8 @@
     sub = lax.broadcasted_iota(I32, (8, CH), 0)
     target = iota_bf16((8, 16, CH), lambda g, s, c: (g * 2 + s // 8) * 2 + s % 2)
 
-    score = split3(score_ref[...])
-    weight = split3(weight_ref[...])
+    score = split3(docs_ref[1])
+    weight = split3(docs_ref[2])
     slot = dest & (DOC - 1)
     zero = jnp.zeros((64, 128), F32)
     fields = (
@@ -109,7 +109,7 @@
     send_ref[...] = (table[0:128] + table[128:256]).reshape(OWNERS, 8, 256)
 
 
-def route(dest, score, weight):
+def route(docs):
     return pl.pallas_call(
         route_body,
         out_shape=(
@@ -117,11 +117,12 @@
             jax.ShapeDtypeStruct((64, 128), I32),
         ),
         scratch_shapes=[pltpu.VMEM((256, DOC), BF16), pltpu.VMEM((256, DOC), BF16)],
-        in_specs=[pl.BlockSpec(memory_space=pltpu.VMEM)] * 3,
+        in_specs=[pl.BlockSpec(memory_space=pltpu.VMEM)],
         out_specs=(pl.BlockSpec(memory_space=pltpu.VMEM), pl.BlockSpec(memory_space=pltpu.VMEM)),
         compiler_params=pltpu.CompilerParams(vmem_limit_bytes=24 << 20),
+        cost_estimate=pl.CostEstimate(flops=2000000000, transcendentals=0, bytes_accessed=10000000),
         name="route",
-    )(dest, score, weight)
+    )(docs)
 
 
 def owner_body(rec_ref, query_ref, clicks_ref, out_ref, a_ref, b_ref, h_ref):
@@ -201,6 +202,7 @@
         in_specs=[pl.BlockSpec(memory_space=pltpu.VMEM)] * 3,
         out_specs=pl.BlockSpec(memory_space=pltpu.VMEM),
         compiler_params=pltpu.CompilerParams(vmem_limit_bytes=24 << 20),
+        cost_estimate=pl.CostEstimate(flops=4000000000, transcendentals=0, bytes_accessed=15000000),
         name="owner",
     )(rec, query, clicks)
 
@@ -284,6 +286,7 @@
         out_shape=jax.ShapeDtypeStruct((OWNERS, F_DEV // 2, 16, 128), BF16),
         scratch_shapes=[pltpu.VMEM((256, DOC), F8), pltpu.VMEM((8, 128), F32)],
         compiler_params=pltpu.CompilerParams(vmem_limit_bytes=40 << 20),
+        cost_estimate=pl.CostEstimate(flops=18000000000, transcendentals=0, bytes_accessed=40000000),
         name="hist",
     )(back, pos, leaf, bins)
 
@@ -313,7 +316,7 @@
 def shards(feature_bins, leaf_index, doc_scores, doc_weights, destination, query_ids, clicks):
     tall = lambda a: a.reshape(64, 128)
     swap = lambda a: lax.all_to_all(a, "rows", split_axis=0, concat_axis=0, tiled=True)
-    send, pos = route(tall(destination), tall(doc_scores), tall(doc_weights))
+    send, pos = route(jnp.stack([tall(destination).astype(F32), tall(doc_scores), tall(doc_weights)]))
     back = owner(swap(send), tall(query_ids), tall(clicks))
     parts = hist(swap(back), pos, tall(leaf_index), feature_bins)
     return total(swap(parts)).reshape(4, F_DEV, 2, BINS)

time: 65.9 us -> 63 us (0.956)
  local copies, waits for them, and re-layouts: 3.52 us -> 0.04 us
  other arithmetic: 0 us -> 0.77 us
    unnamed x14 -> x12, local copies, waits for them, and re-layouts: 3.52 us -> 0.04 us
    convert_element_type x0 -> x1, other arithmetic: none -> 0.77 us  [shards(): tall(destination).astype(F32)]
where the time goes in v4:
time: 63 us; the launch traced here: 62.6 us
  blocking collectives  43.7 us (69%)
  Pallas kernels  18.1 us (29%)
  other arithmetic  0.77 us (1%)
    all_to_all x3, blocking collectives, shards(): lax.all_to_all(a, 'rows', split_axis=0, concat_axis=0, tiled=True)  43.7 us
    pallas_call x1, Pallas kernels, hist(): pl.pallas_call(hist_body, grid=(F_DEV // GF,), in_specs=[whole(back), who...  11 us
    pallas_call x1, Pallas kernels, owner(): pl.pallas_call(owner_body, out_shape=jax.ShapeDtypeStruct((OWNERS, 8, 128...  4.33 us
    pallas_call x1, Pallas kernels, route(): pl.pallas_call(route_body, out_shape=(jax.ShapeDtypeStruct((OWNERS, 8, 25...  1.91 us

profile of v4, /device:TPU:160, one launch (start us, length us, event | category | flops | bytes accessed | tf_op | source)
XLA Modules:
  0.0 62.6 jit_solution(16078588584050879816)
XLA Ops:
  0.0 0.0 copy-start.4
  0.0 0.0 copy-start.5
  0.0 0.8 %convert_bitcast_fusion = f32[1,64,128]{2,1,0:T(8,128)S(1)} fusion(s32[8192]{0:T(1024)} %param.11), kind=kLoop, calls=%fused_computation.1 | loop fusion | flops 8192 | bytes 65536 | tf_op jit(solution)/shard_map/convert_element_type | solution.py:319
  0.8 0.0 copy-done.4
  0.8 0.0 copy-done.5
  0.8 1.9 %route.1 = (f32[16,8,256]{2,1,0:T(8,128)S(1)}, s32[64,128]{1,0:T(8,128)S(1)}) custom-call(f32[3,64,128]{2,1,0:T(8,128)S(1)} %pad_maximum_fusion.docs_ref), custom_call_target="tpu_custom_call" | custom-call | flops 2000000000 | bytes 10000000 | tf_op jit(solution)/shard_map/route/pallas_call | solution.py:113
  2.7 0.0 copy-start.1
  2.7 0.0 copy-start.2
  2.7 14.8 %all_to_all.15.rec_ref = f32[16,8,256]{2,1,0:T(8,128)S(1)} all-to-all(f32[16,8,256]{2,1,0:T(8,128)S(1)} %get-tuple-element.7), channel_id=1, replica_groups=mesh['rows'=16,'feat'=16] {'rows'}, dimensions={0} | all-to-all | bytes 262144 | tf_op jit(solution)/shard_map/all_to_all | solution.py:318
  17.6 0.0 copy-done.1
  17.6 0.0 copy-done.2
  17.6 0.0 copy-start
  17.6 4.3 %owner.1 = f32[16,8,128]{2,1,0:T(8,128)S(1)} custom-call(f32[16,8,256]{2,1,0:T(8,128)S(1)} %all_to_all.15.rec_ref, s32[64,128]{1,0:T(8,128)S(1)} %bitcast.8, s32[64,128]{1,0:T(8,128)S(1)} %bitcast.9), custom_call_target="tpu_custom_call" | custom-call | flops 4000000000 | bytes 15000000 | tf_op jit(solution)/shard_map/owner/pallas_call | solution.py:194
  21.9 0.0 copy-start.3
  21.9 10.7 %all_to_all.16.back_ref = f32[16,8,128]{2,1,0:T(8,128)S(1)} all-to-all(f32[16,8,128]{2,1,0:T(8,128)S(1)} %owner.1), channel_id=1, replica_groups=mesh['rows'=16,'feat'=16] {'rows'}, dimensions={0} | all-to-all | bytes 131072 | tf_op jit(solution)/shard_map/all_to_all | solution.py:318
  32.7 0.0 copy-done
  32.7 0.0 copy-done.3
  32.7 11.0 %hist.1 = bf16[16,16,16,128]{3,2,1,0:T(8,128)(2,1)S(1)} custom-call(f32[16,8,128]{2,1,0:T(8,128)S(1)} %all_to_all.16.back_ref, s32[64,128]{1,0:T(8,128)S(1)} %get-tuple-element.8.pos_ref, s32[64,128]{1,0:T(8,128)S(1)} %bitcast.10, s32[32,8192]{1,0:T(8,128)S(1)} %copy-done), custom_call_target="tpu_custom_call" | custom-call | flops 17999998976 | bytes 40000000 | tf_op jit(solution)/shard_map/hist/pallas_call | solution.py:281
  43.7 18.1 %all_to_all.17.rec_ref = bf16[16,16,16,128]{3,2,1,0:T(8,128)(2,1)S(1)} all-to-all(bf16[16,16,16,128]{3,2,1,0:T(8,128)(2,1)S(1)} %hist.1), channel_id=1, replica_groups=mesh['rows'=16,'feat'=16] {'rows'}, dimensions={0} | all-to-all | bytes 2097152 | tf_op jit(solution)/shard_map/all_to_all | solution.py:318
  61.7 0.9 %total.1 = f32[4,64,128]{2,1,0:T(8,128)} custom-call(bf16[16,16,16,128]{3,2,1,0:T(8,128)(2,1)S(1)} %all_to_all.17.rec_ref), custom_call_target="tpu_custom_call" | custom-call | tf_op jit(solution)/shard_map/total/pallas_call | solution.py:305
  (1 shorter events, 0.0 us)
Async XLA Ops:
  0.0 0.8 %copy-start.4 = (f32[8192]{0:T(1024)S(1)}, f32[8192]{0:T(1024)}, u32[]{:S(2)}) copy-start(f32[8192]{0:T(1024)} %param.10) | copy-start | bytes 98308
  0.0 0.8 %copy-start.5 = (f32[8192]{0:T(1024)S(1)}, f32[8192]{0:T(1024)}, u32[]{:S(2)}) copy-start(f32[8192]{0:T(1024)} %param.9) | copy-start | bytes 98308
  2.7 14.9 %copy-start.1 = (s32[8192]{0:T(1024)S(1)}, s32[8192]{0:T(1024)}, u32[]{:S(2)}) copy-start(s32[8192]{0:T(1024)} %param.12) | copy-start | bytes 98308
  2.7 14.8 %copy-start.2 = (s32[8192]{0:T(1024)S(1)}, s32[8192]{0:T(1024)}, u32[]{:S(2)}) copy-start(s32[8192]{0:T(1024)} %param.13) | copy-start | bytes 98308
  17.6 15.1 %copy-start = (s32[32,8192]{1,0:T(8,128)S(1)}, s32[32,8192]{1,0:T(8,128)}, u32[]{:S(2)}) copy-start(s32[32,8192]{1,0:T(8,128)} %bins_ref.1) | copy-start | bytes 3145732
  21.9 10.8 %copy-start.3 = (s32[8192]{0:T(1024)S(1)}, s32[8192]{0:T(1024)}, u32[]{:S(2)}) copy-start(s32[8192]{0:T(1024)} %param.8) | copy-start | bytes 98308

commit v5 on v4

--- a/solution.py
+++ b/solution.py
@@ -219,72 +219,74 @@
     return jnp.where(it == r[None], jnp.ones((), F8), jnp.zeros((), F8)).reshape(128, cols)
 
 
-def hist_body(back_ref, pos_ref, leaf_ref, bins_ref, send_ref, spread_ref, down_ref):
-    @pl.when(pl.program_id(0) == 0)
-    def _():
-        back = back_ref[...].reshape(128, 128)
-        table = back.astype(BF16)
-        sub8 = lax.broadcasted_iota(I32, (8, 128), 0)
-        peak = jnp.max(jnp.abs(back_ref[...]), axis=0)
-        peak = jnp.max(peak, axis=1, keepdims=True)
-        odd = lax.broadcasted_iota(I32, (8, 1), 0) % 2
-        top0 = jnp.max(jnp.where(odd == 0, peak, 0.0), axis=0, keepdims=True)
-        top1 = jnp.max(jnp.where(odd == 1, peak, 0.0), axis=0, keepdims=True)
-        top = jnp.where(odd == 0, top0, top1)
-        up = jnp.full((8, 1), 2.0**-20, F32)
-        down = jnp.full((8, 1), 2.0**20, F32)
-        for e in (64, 32, 16, 8, 4, 2, 1):
-            fits = top * (up * 2.0**e) <= 448.0
-            up = jnp.where(fits, up * 2.0**e, up)
-            down = jnp.where(fits, down * 2.0**-e, down)
-        up = jnp.broadcast_to(up, (8, CH))
-
-        for t in range(DOC // CH):
-            rows = slice(t * 8, t * 8 + 8)
-            pos = lanes(pos_ref[rows, :])
-            leaf = lanes(leaf_ref[rows, :])
-            picked = nn(table, one_hot(pos & 127, 128, CH))
-            hi = jnp.broadcast_to(pos >> 7, (8, CH))
-            quarter = lax.broadcasted_iota(I32, (8, CH), 0) // 2
-            acc = jnp.zeros((8, CH), F32)
-            for o in range(OWNERS):
-                acc = acc + jnp.where(hi == quarter + 4 * o, picked[o * 8 : (o + 1) * 8], 0.0)
-            acc = acc + pltpu.roll(acc, 4, 0)
-            acc = acc + pltpu.roll(acc, 2, 0)
-            acc = acc * up
-            high = acc.astype(F8).astype(F32)
-            low = (acc - high) * LOW
-            it = iota_bf16((8, 16, CH), lambda g, s, c: g * 8 + s // 2)
-            hit = it == rows16(leaf)[None]
-            for n, v in enumerate((high, low)):
-                both = jnp.concatenate([v, v], axis=0).astype(BF16)
-                spread_ref[n * 128 : (n + 1) * 128, t * CH : t * CH + CH] = (
-                    jnp.where(hit, both[None], jnp.zeros((), BF16)).reshape(128, CH).astype(F8)
-                )
-        down_ref[...] = jnp.broadcast_to(down, (8, 128))
-
-    scale = down_ref[...][None]
-    hot = jnp.concatenate([one_hot8(bins_ref[j : j + 1, :], DOC) for j in range(GF)], axis=0)
-    acc = nt(spread_ref[...], hot)
-    acc = acc[:128] + acc[128:] * (1.0 / LOW)
-    cut = [
-        (acc[:, 128 * j : 128 * j + 128].reshape(OWNERS, 8, 128) * scale).reshape(OWNERS, 1, 8, 128)
-        for j in range(GF)
-    ]
-    send_ref[...] = (
-        jnp.concatenate(cut, axis=1).reshape(OWNERS, GF // 2, 16, 128).astype(BF16)
-    )
+def hist_body(back_ref, pos_ref, leaf_ref, bins_ref, send_ref, spread_ref):
+    back = back_ref[...].reshape(128, 128)
+    table = back.astype(BF16)
+    sub8 = lax.broadcasted_iota(I32, (8, 128), 0)
+    peak = jnp.max(jnp.abs(back_ref[...]), axis=0)
+    peak = jnp.max(peak, axis=1, keepdims=True)
+    odd = lax.broadcasted_iota(I32, (8, 1), 0) % 2
+    top0 = jnp.max(jnp.where(odd == 0, peak, 0.0), axis=0, keepdims=True)
+    top1 = jnp.max(jnp.where(odd == 1, peak, 0.0), axis=0, keepdims=True)
+    top = jnp.where(odd == 0, top0, top1)
+    up = jnp.full((8, 1), 2.0**-20, F32)
+    down = jnp.full((8, 1), 2.0**20, F32)
+    for e in (64, 32, 16, 8, 4, 2, 1):
+        fits = top * (up * 2.0**e) <= 448.0
+        up = jnp.where(fits, up * 2.0**e, up)
+        down = jnp.where(fits, down * 2.0**-e, down)
+    up = jnp.broadcast_to(up, (8, CH))
+
+    for t in range(DOC // CH):
+        rows = slice(t * 8, t * 8 + 8)
+        pos = lanes(pos_ref[rows, :])
+        leaf = lanes(leaf_ref[rows, :])
+        picked = nn(table, one_hot(pos & 127, 128, CH))
+        hi = jnp.broadcast_to(pos >> 7, (8, CH))
+        quarter = lax.broadcasted_iota(I32, (8, CH), 0) // 2
+        acc = jnp.zeros((8, CH), F32)
+        for o in range(OWNERS):
+            acc = acc + jnp.where(hi == quarter + 4 * o, picked[o * 8 : (o + 1) * 8], 0.0)
+        acc = acc + pltpu.roll(acc, 4, 0)
+        acc = acc + pltpu.roll(acc, 2, 0)
+        acc = acc * up
+        high = acc.astype(F8).astype(F32)
+        low = (acc - high) * LOW
+        it = iota_bf16((8, 16, CH), lambda g, s, c: g * 8 + s // 2)
+        hit = it == rows16(leaf)[None]
+        for n, v in enumerate((high, low)):
+            both = jnp.concatenate([v, v], axis=0).astype(BF16)
+            spread_ref[n * 128 : (n + 1) * 128, t * CH : t * CH + CH] = (
+                jnp.where(hit, both[None], jnp.zeros((), BF16)).reshape(128, CH).astype(F8)
+            )
+    scale = jnp.broadcast_to(down, (8, 128))[None]
+
+    def group(p, carry):
+        tile = bins_ref[pl.ds(p * GF, GF), :]
+        hot = jnp.concatenate([one_hot8(tile[j : j + 1, :], DOC) for j in range(GF)], axis=0)
+        acc = nt(spread_ref[...], hot)
+        acc = acc[:128] + acc[128:] * (1.0 / LOW)
+        cut = [
+            (acc[:, 128 * j : 128 * j + 128].reshape(OWNERS, 8, 128) * scale).reshape(OWNERS, 1, 8, 128)
+            for j in range(GF)
+        ]
+        send_ref[:, pl.ds(p * (GF // 2), GF // 2)] = (
+            jnp.concatenate(cut, axis=1).reshape(OWNERS, GF // 2, 16, 128).astype(BF16)
+        )
+        return carry
+
+    for p in range(F_DEV // GF):
+        group(p, 0)
 
 
 def hist(back, pos, leaf, bins):
-    whole = lambda a: pl.BlockSpec(a.shape, lambda p: (0,) * a.ndim)
+    vmem = pl.BlockSpec(memory_space=pltpu.VMEM)
     return pl.pallas_call(
         hist_body,
-        grid=(F_DEV // GF,),
-        in_specs=[whole(back), whole(pos), whole(leaf), pl.BlockSpec((GF, DOC), lambda p: (p, 0))],
-        out_specs=pl.BlockSpec((OWNERS, GF // 2, 16, 128), lambda p: (0, p, 0, 0)),
+        in_specs=[vmem] * 4,
+        out_specs=vmem,
         out_shape=jax.ShapeDtypeStruct((OWNERS, F_DEV // 2, 16, 128), BF16),
-        scratch_shapes=[pltpu.VMEM((256, DOC), F8), pltpu.VMEM((8, 128), F32)],
+        scratch_shapes=[pltpu.VMEM((256, DOC), F8)],
         compiler_params=pltpu.CompilerParams(vmem_limit_bytes=40 << 20),
         cost_estimate=pl.CostEstimate(flops=18000000000, transcendentals=0, bytes_accessed=40000000),
         name="hist",

time: 63 us -> 61.9 us (0.983)
  Pallas kernels: 18.1 us -> 17 us
    pallas_call x1, Pallas kernels: 11 us -> 9.86 us  [hist(): pl.pallas_call(hist_body, in_specs=[vmem] * 4, out_specs=vmem, out_shape=...]
where the time goes in v5:
time: 61.9 us; the launch traced here: 61.5 us
  blocking collectives  43.7 us (71%)
  Pallas kernels  17 us (27%)
  other arithmetic  0.77 us (1%)
    all_to_all x3, blocking collectives, shards(): lax.all_to_all(a, 'rows', split_axis=0, concat_axis=0, tiled=True)  43.7 us
    pallas_call x1, Pallas kernels, hist(): pl.pallas_call(hist_body, in_specs=[vmem] * 4, out_specs=vmem, out_shape=...  9.86 us
    pallas_call x1, Pallas kernels, owner(): pl.pallas_call(owner_body, out_shape=jax.ShapeDtypeStruct((OWNERS, 8, 128...  4.33 us
    pallas_call x1, Pallas kernels, route(): pl.pallas_call(route_body, out_shape=(jax.ShapeDtypeStruct((OWNERS, 8, 25...  1.91 us

profile of v5, /device:TPU:160, one launch (start us, length us, event | category | flops | bytes accessed | tf_op | source)
XLA Modules:
  0.0 61.5 jit_solution(7648270292580796905)
XLA Ops:
  0.0 0.0 copy-start.4
  0.0 0.0 copy-start.5
  0.0 0.8 %convert_bitcast_fusion = f32[1,64,128]{2,1,0:T(8,128)S(1)} fusion(s32[8192]{0:T(1024)} %param.11), kind=kLoop, calls=%fused_computation.1 | loop fusion | flops 8192 | bytes 65536 | tf_op jit(solution)/shard_map/convert_element_type | solution.py:321
  0.8 0.0 copy-done.4
  0.8 0.0 copy-done.5
  0.8 1.9 %route.1 = (f32[16,8,256]{2,1,0:T(8,128)S(1)}, s32[64,128]{1,0:T(8,128)S(1)}) custom-call(f32[3,64,128]{2,1,0:T(8,128)S(1)} %pad_maximum_fusion.docs_ref), custom_call_target="tpu_custom_call" | custom-call | flops 2000000000 | bytes 10000000 | tf_op jit(solution)/shard_map/route/pallas_call | solution.py:113
  2.7 0.0 copy-start.1
  2.7 0.0 copy-start.2
  2.7 14.8 %all_to_all.15.rec_ref = f32[16,8,256]{2,1,0:T(8,128)S(1)} all-to-all(f32[16,8,256]{2,1,0:T(8,128)S(1)} %get-tuple-element.7), channel_id=1, replica_groups=mesh['rows'=16,'feat'=16] {'rows'}, dimensions={0} | all-to-all | bytes 262144 | tf_op jit(solution)/shard_map/all_to_all | solution.py:320
  17.6 0.0 copy-done.1
  17.6 0.0 copy-done.2
  17.6 0.0 copy-start
  17.6 4.3 %owner.1 = f32[16,8,128]{2,1,0:T(8,128)S(1)} custom-call(f32[16,8,256]{2,1,0:T(8,128)S(1)} %all_to_all.15.rec_ref, s32[64,128]{1,0:T(8,128)S(1)} %bitcast.8, s32[64,128]{1,0:T(8,128)S(1)} %bitcast.9), custom_call_target="tpu_custom_call" | custom-call | flops 4000000000 | bytes 15000000 | tf_op jit(solution)/shard_map/owner/pallas_call | solution.py:194
  21.9 0.0 copy-start.3
  21.9 10.7 %all_to_all.16.back_ref = f32[16,8,128]{2,1,0:T(8,128)S(1)} all-to-all(f32[16,8,128]{2,1,0:T(8,128)S(1)} %owner.1), channel_id=1, replica_groups=mesh['rows'=16,'feat'=16] {'rows'}, dimensions={0} | all-to-all | bytes 131072 | tf_op jit(solution)/shard_map/all_to_all | solution.py:320
  32.7 0.0 copy-done
  32.7 0.0 copy-done.3
  32.7 9.9 %hist.1 = bf16[16,16,16,128]{3,2,1,0:T(8,128)(2,1)S(1)} custom-call(f32[16,8,128]{2,1,0:T(8,128)S(1)} %all_to_all.16.back_ref, s32[64,128]{1,0:T(8,128)S(1)} %get-tuple-element.8.pos_ref, s32[64,128]{1,0:T(8,128)S(1)} %bitcast.10, s32[32,8192]{1,0:T(8,128)S(1)} %copy-done), custom_call_target="tpu_custom_call" | custom-call | flops 17999998976 | bytes 40000000 | tf_op jit(solution)/shard_map/hist/pallas_call | solution.py:284
  42.5 18.1 %all_to_all.17.rec_ref = bf16[16,16,16,128]{3,2,1,0:T(8,128)(2,1)S(1)} all-to-all(bf16[16,16,16,128]{3,2,1,0:T(8,128)(2,1)S(1)} %hist.1), channel_id=1, replica_groups=mesh['rows'=16,'feat'=16] {'rows'}, dimensions={0} | all-to-all | bytes 2097152 | tf_op jit(solution)/shard_map/all_to_all | solution.py:320
  60.6 0.9 %total.1 = f32[4,64,128]{2,1,0:T(8,128)} custom-call(bf16[16,16,16,128]{3,2,1,0:T(8,128)(2,1)S(1)} %all_to_all.17.rec_ref), custom_call_target="tpu_custom_call" | custom-call | tf_op jit(solution)/shard_map/total/pallas_call | solution.py:307
  (1 shorter events, 0.0 us)
Async XLA Ops:
  0.0 0.8 %copy-start.4 = (f32[8192]{0:T(1024)S(1)}, f32[8192]{0:T(1024)}, u32[]{:S(2)}) copy-start(f32[8192]{0:T(1024)} %param.10) | copy-start | bytes 98308
  0.0 0.8 %copy-start.5 = (f32[8192]{0:T(1024)S(1)}, f32[8192]{0:T(1024)}, u32[]{:S(2)}) copy-start(f32[8192]{0:T(1024)} %param.9) | copy-start | bytes 98308
  2.7 14.8 %copy-start.1 = (s32[8192]{0:T(1024)S(1)}, s32[8192]{0:T(1024)}, u32[]{:S(2)}) copy-start(s32[8192]{0:T(1024)} %param.12) | copy-start | bytes 98308
  2.7 14.8 %copy-start.2 = (s32[8192]{0:T(1024)S(1)}, s32[8192]{0:T(1024)}, u32[]{:S(2)}) copy-start(s32[8192]{0:T(1024)} %param.13) | copy-start | bytes 98308
  17.6 15.1 %copy-start = (s32[32,8192]{1,0:T(8,128)S(1)}, s32[32,8192]{1,0:T(8,128)}, u32[]{:S(2)}) copy-start(s32[32,8192]{1,0:T(8,128)} %bins_ref.1) | copy-start | bytes 3145732
  21.9 10.8 %copy-start.3 = (s32[8192]{0:T(1024)S(1)}, s32[8192]{0:T(1024)}, u32[]{:S(2)}) copy-start(s32[8192]{0:T(1024)} %param.8) | copy-start | bytes 98308

commit v6 on v5

--- a/solution.py
+++ b/solution.py
@@ -209,7 +209,7 @@
 
 F8 = jnp.float8_e4m3fn
 LOW = 16.0
-GF = 8
+GF = 16
 PB = 8
 
 

time: 61.9 us -> 61.9 us (level)
  no operation moved by 1% of the time
where the time goes in v6:
time: 61.9 us; the launch traced here: 61.5 us
  blocking collectives  43.7 us (71%)
  Pallas kernels  17 us (27%)
  other arithmetic  0.77 us (1%)
    all_to_all x3, blocking collectives, shards(): lax.all_to_all(a, 'rows', split_axis=0, concat_axis=0, tiled=True)  43.7 us
    pallas_call x1, Pallas kernels, hist(): pl.pallas_call(hist_body, in_specs=[vmem] * 4, out_specs=vmem, out_shape=...  9.86 us
    pallas_call x1, Pallas kernels, owner(): pl.pallas_call(owner_body, out_shape=jax.ShapeDtypeStruct((OWNERS, 8, 128...  4.33 us
    pallas_call x1, Pallas kernels, route(): pl.pallas_call(route_body, out_shape=(jax.ShapeDtypeStruct((OWNERS, 8, 25...  1.91 us

profile of v6, /device:TPU:160, one launch (start us, length us, event | category | flops | bytes accessed | tf_op | source)
XLA Modules:
  0.0 61.5 jit_solution(7648270292580796905)
XLA Ops:
  0.0 0.0 copy-start.4
  0.0 0.0 copy-start.5
  0.0 0.8 %convert_bitcast_fusion = f32[1,64,128]{2,1,0:T(8,128)S(1)} fusion(s32[8192]{0:T(1024)} %param.11), kind=kLoop, calls=%fused_computation.1 | loop fusion | flops 8192 | bytes 65536 | tf_op jit(solution)/shard_map/convert_element_type | solution.py:321
  0.8 0.0 copy-done.4
  0.8 0.0 copy-done.5
  0.8 1.9 %route.1 = (f32[16,8,256]{2,1,0:T(8,128)S(1)}, s32[64,128]{1,0:T(8,128)S(1)}) custom-call(f32[3,64,128]{2,1,0:T(8,128)S(1)} %pad_maximum_fusion.docs_ref), custom_call_target="tpu_custom_call" | custom-call | flops 2000000000 | bytes 10000000 | tf_op jit(solution)/shard_map/route/pallas_call | solution.py:113
  2.7 0.0 copy-start.1
  2.7 0.0 copy-start.2
  2.7 14.8 %all_to_all.15.rec_ref = f32[16,8,256]{2,1,0:T(8,128)S(1)} all-to-all(f32[16,8,256]{2,1,0:T(8,128)S(1)} %get-tuple-element.7), channel_id=1, replica_groups=mesh['rows'=16,'feat'=16] {'rows'}, dimensions={0} | all-to-all | bytes 262144 | tf_op jit(solution)/shard_map/all_to_all | solution.py:320
  17.6 0.0 copy-done.1
  17.6 0.0 copy-done.2
  17.6 0.0 copy-start
  17.6 4.3 %owner.1 = f32[16,8,128]{2,1,0:T(8,128)S(1)} custom-call(f32[16,8,256]{2,1,0:T(8,128)S(1)} %all_to_all.15.rec_ref, s32[64,128]{1,0:T(8,128)S(1)} %bitcast.8, s32[64,128]{1,0:T(8,128)S(1)} %bitcast.9), custom_call_target="tpu_custom_call" | custom-call | flops 4000000000 | bytes 15000000 | tf_op jit(solution)/shard_map/owner/pallas_call | solution.py:194
  21.9 0.0 copy-start.3
  21.9 10.7 %all_to_all.16.back_ref = f32[16,8,128]{2,1,0:T(8,128)S(1)} all-to-all(f32[16,8,128]{2,1,0:T(8,128)S(1)} %owner.1), channel_id=1, replica_groups=mesh['rows'=16,'feat'=16] {'rows'}, dimensions={0} | all-to-all | bytes 131072 | tf_op jit(solution)/shard_map/all_to_all | solution.py:320
  32.7 0.0 copy-done
  32.7 0.0 copy-done.3
  32.7 9.9 %hist.1 = bf16[16,16,16,128]{3,2,1,0:T(8,128)(2,1)S(1)} custom-call(f32[16,8,128]{2,1,0:T(8,128)S(1)} %all_to_all.16.back_ref, s32[64,128]{1,0:T(8,128)S(1)} %get-tuple-element.8.pos_ref, s32[64,128]{1,0:T(8,128)S(1)} %bitcast.10, s32[32,8192]{1,0:T(8,128)S(1)} %copy-done), custom_call_target="tpu_custom_call" | custom-call | flops 17999998976 | bytes 40000000 | tf_op jit(solution)/shard_map/hist/pallas_call | solution.py:284
  42.5 18.1 %all_to_all.17.rec_ref = bf16[16,16,16,128]{3,2,1,0:T(8,128)(2,1)S(1)} all-to-all(bf16[16,16,16,128]{3,2,1,0:T(8,128)(2,1)S(1)} %hist.1), channel_id=1, replica_groups=mesh['rows'=16,'feat'=16] {'rows'}, dimensions={0} | all-to-all | bytes 2097152 | tf_op jit(solution)/shard_map/all_to_all | solution.py:320
  60.6 0.9 %total.1 = f32[4,64,128]{2,1,0:T(8,128)} custom-call(bf16[16,16,16,128]{3,2,1,0:T(8,128)(2,1)S(1)} %all_to_all.17.rec_ref), custom_call_target="tpu_custom_call" | custom-call | tf_op jit(solution)/shard_map/total/pallas_call | solution.py:307
  (1 shorter events, 0.0 us)
Async XLA Ops:
  0.0 0.8 %copy-start.4 = (f32[8192]{0:T(1024)S(1)}, f32[8192]{0:T(1024)}, u32[]{:S(2)}) copy-start(f32[8192]{0:T(1024)} %param.10) | copy-start | bytes 98308
  0.0 0.8 %copy-start.5 = (f32[8192]{0:T(1024)S(1)}, f32[8192]{0:T(1024)}, u32[]{:S(2)}) copy-start(f32[8192]{0:T(1024)} %param.9) | copy-start | bytes 98308
  2.7 14.8 %copy-start.1 = (s32[8192]{0:T(1024)S(1)}, s32[8192]{0:T(1024)}, u32[]{:S(2)}) copy-start(s32[8192]{0:T(1024)} %param.12) | copy-start | bytes 98308
  2.7 14.8 %copy-start.2 = (s32[8192]{0:T(1024)S(1)}, s32[8192]{0:T(1024)}, u32[]{:S(2)}) copy-start(s32[8192]{0:T(1024)} %param.13) | copy-start | bytes 98308
  17.6 15.1 %copy-start = (s32[32,8192]{1,0:T(8,128)S(1)}, s32[32,8192]{1,0:T(8,128)}, u32[]{:S(2)}) copy-start(s32[32,8192]{1,0:T(8,128)} %bins_ref.1) | copy-start | bytes 3145732
  21.9 10.8 %copy-start.3 = (s32[8192]{0:T(1024)S(1)}, s32[8192]{0:T(1024)}, u32[]{:S(2)}) copy-start(s32[8192]{0:T(1024)} %param.8) | copy-start | bytes 98308
